TPU v7x, 128 devices: a whole 4x4x4 slice. The times are simulated.
128 devices in a mesh: fibre: 8 (over z, core), blk: 16 (over x, y).
Axes of the slice: x: 4, y: 4, z: 4, core: 2. Of those that a mesh axis runs over, the one named last changes fastest.
Arguments:
- readings: bfloat16 [524288, 1024], P(('fibre', 'blk')), as said below
- values: bfloat16 [524288], P(('fibre', 'blk')), may hold values from -6 to 6
- counts: int32 [128], P(('fibre', 'blk')), may hold values from 1 to 4096, as said below
- prior_root: float32 [1024, 1024], P(('fibre', 'blk')), as said below
- prior_info: float32 [1024], P(('fibre', 'blk')), may hold values from -6 to 6
Outputs:
- post_root: float32 [1024, 1024], P('blk')
- post_info: float32 [1024], replicated
Inputs may be any that keep to these rules, and one draw needn't show every extreme that they name: `counts`: every owner has at least one live row, and in every draw some owner has all 4096 rows live. `prior_root`: upper triangular with a positive diagonal. `readings`: whitened measurement rows; nothing beyond the stated range is promised.
All inputs are finite; a program needn't handle non-finite values.
Results may differ from a plain program's by a relative error of at most 0.0003.
Values sent between devices are 32-bit elements; how exact they have to be, the bound alone decides.
A program may use at most 128 MiB of HBM per device.

v0:
```python
import jax
import jax.numpy as jnp
from jax import lax
from jax.sharding import PartitionSpec as P


def accumulate(row_data, val_data, active, state_width):
    block_rows = min(512, row_data.shape[0])
    block_count = (active + block_rows - 1) // block_rows

    def add_block(turn_index, totals):
        row_piece = lax.dynamic_slice_in_dim(row_data, turn_index * block_rows, block_rows, 0)
        val_piece = lax.dynamic_slice_in_dim(val_data, turn_index * block_rows, block_rows, 0)
        gram_part = lax.dot_general(
            row_piece, row_piece, (((0,), (0,)), ((), ())), preferred_element_type=jnp.float32
        )
        info_part = jnp.dot(val_piece, row_piece, preferred_element_type=jnp.float32)
        return (totals[0] + gram_part, totals[1] + info_part)

    initial = (
        jnp.zeros((state_width, state_width), jnp.float32),
        jnp.zeros((state_width,), jnp.float32),
    )
    return lax.fori_loop(0, block_count, add_block, initial)


def local(readings, values, counts, prior_root, prior_info):
    capacity, state_width = readings.shape
    own_count = counts[0]
    live_mask = jnp.arange(capacity, dtype=jnp.int32) < own_count
    masked_rows = jnp.where(live_mask[:, None], readings, jnp.zeros((), readings.dtype))
    masked_vals = jnp.where(live_mask, values, jnp.zeros((), values.dtype))
    gram_local, info_local = accumulate(masked_rows, masked_vals, own_count, state_width)
    gram_local = gram_local + jnp.dot(prior_root.T, prior_root, precision=lax.Precision.HIGHEST)
    info_local = info_local + jnp.dot(prior_info, prior_root, precision=lax.Precision.HIGHEST)
    total_gram, total_info = lax.psum((gram_local, info_local), ("fibre", "blk"))
    factor = jnp.linalg.cholesky(total_gram)
    post_info = lax.linalg.triangular_solve(
        factor, total_info[:, None], left_side=True, lower=True
    )[:, 0]
    row_count = state_width // lax.axis_size("blk")
    post_root = lax.dynamic_slice_in_dim(factor.T, lax.axis_index("blk") * row_count, row_count, 0)
    return (post_root, post_info)


def solution(mesh):
    placed = (
        P(("fibre", "blk"), None),
        P(("fibre", "blk")),
        P(("fibre", "blk")),
        P(("fibre", "blk"), None),
        P(("fibre", "blk")),
    )
    return jax.shard_map(
        local, mesh=mesh, in_specs=placed, out_specs=(P("blk", None), P()), check_vma=False
    )
```

profile of v0, /device:TPU:1, one launch (start us, length us, event | category | flops | bytes accessed | tf_op | source)
XLA Modules:
  0.0 591.6 jit_solution(17716149881141357799)
XLA Ops:
  7.9 7.2 %broadcast_select_fusion = bf16[4096,1024]{1,0:T(8,128)(2,1)} fusion(bf16[4096,1024]{1,0:T(8,128)(2,1)} %param.7, pred[4096]{0:T(1024)(128)(4,1)S(1)} %iota_compare_fusion.3), kind=kLoop, calls=%fused_computation.8 | loop fusion | flops 4194304 | bytes 16781312 | tf_op jit(solution)/shard_map/jit(_where)/select_n | solution.py:31
  15.2 2.5 broadcast_in_dim.26
  17.7 30.7 %while.13 = (s32[]{:T(128)}, f32[1024,1024]{1,0:T(8,128)}, f32[1024]{0:T(1024)S(1)}, s32[]{:T(128)}, bf16[4096,1024]{1,0:T(8,128)(2,1)}, /*index=5*/bf16[4096]{0...) while((s32[]{:T(128)}, f32[1024,1024]{1,0:T(8,128)}, f32[1024]{0:T(1024)S(1)}, s32[]{:T(128)}, ...), condition=%wide.region_1.2_spmd, body=%wide.region_0.1_spmd.sunk | while | flops 1075840000 | bytes 10507423 | solution.py:24
  19.2 6.1 %convolution_add_fusion.3 = f32[1024,1024]{1,0:T(8,128)} fusion(f32[1024,1024]{1,0:T(8,128)} %get-tuple-element.203, bf16[4096,1024]{1,0:T(8,128)(2,1)} %get-tuple-element.216, s32[]{:T(128)S(6)} %select_n.34), kind=kOutput, calls=%fused_computation.clone.1 | convolution fusion | flops 1074790400 | bytes 9437188 | tf_op jit(solution)/shard_map/while/body/dot_general | solution.py:14
  26.9 6.1 %convolution_add_fusion.3 = f32[1024,1024]{1,0:T(8,128)} fusion(f32[1024,1024]{1,0:T(8,128)} %get-tuple-element.203, bf16[4096,1024]{1,0:T(8,128)(2,1)} %get-tuple-element.216, s32[]{:T(128)S(6)} %select_n.34), kind=kOutput, calls=%fused_computation.clone.1 | convolution fusion | flops 1074790400 | bytes 9437188 | tf_op jit(solution)/shard_map/while/body/dot_general | solution.py:14
  34.6 6.1 %convolution_add_fusion.3 = f32[1024,1024]{1,0:T(8,128)} fusion(f32[1024,1024]{1,0:T(8,128)} %get-tuple-element.203, bf16[4096,1024]{1,0:T(8,128)(2,1)} %get-tuple-element.216, s32[]{:T(128)S(6)} %select_n.34), kind=kOutput, calls=%fused_computation.clone.1 | convolution fusion | flops 1074790400 | bytes 9437188 | tf_op jit(solution)/shard_map/while/body/dot_general | solution.py:14
  42.2 6.2 %convolution_add_fusion.3 = f32[1024,1024]{1,0:T(8,128)} fusion(f32[1024,1024]{1,0:T(8,128)} %get-tuple-element.203, bf16[4096,1024]{1,0:T(8,128)(2,1)} %get-tuple-element.216, s32[]{:T(128)S(6)} %select_n.34), kind=kOutput, calls=%fused_computation.clone.1 | convolution fusion | flops 1074790400 | bytes 9437188 | tf_op jit(solution)/shard_map/while/body/dot_general | solution.py:14
  48.4 5.3 copy.7
  53.8 6.6 %convolution_add_fusion.1 = f32[1024,1024]{0,1:T(8,128)} fusion(f32[1024,1024]{0,1:T(8,128)} %copy.7, f32[8,1024]{1,0:T(8,128)S(1)} %copy-done), kind=kOutput, calls=%fused_computation.14 | convolution fusion | flops 101711872 | bytes 8421376 | tf_op jit(solution)/shard_map/dot_general | solution.py:34
  61.2 98.6 %psum.15 = f32[1024]{0:T(1024)S(1)} all-reduce(f32[1024]{0:T(1024)S(1)} %add.110), channel_id=1, replica_groups=mesh['fibre'=8,'blk'=16] {'fibre','blk'}, use_global_device_ids=true, to_apply=%region_19.20 | all-reduce | flops 1024 | bytes 8192 | tf_op jit(solution)/shard_map/psum | solution.py:36
  159.9 87.6 %all-reduce.3.cloned.1.call-done = f32[1024,1024]{0,1:T(8,128)} async-done(((f32[1024,1024]{0,1:T(8,128)}), f32[1024,1024]{0,1:T(8,128)}) %all-reduce.3.cloned.1.call-update) | async-done | bytes 4194320 | tf_op jit(solution)/shard_map/psum | solution.py:36
  247.4 5.8 copy.9
  253.2 4.4 fusion.5
  259.6 11.7 %cholesky.222 = f32[128,128]{1,0:T(8,128)S(1)} custom-call(f32[128,128]{1,0:T(8,128)S(1)} %cholesky.577), custom_call_target="Cholesky" | custom-call | tf_op jit(solution)/shard_map/jit(cholesky)/cholesky | solution.py:37
  271.3 2.5 cholesky.254
  273.8 9.8 %custom-call.62 = f32[1,128,128]{1,2,0:T(8,128)S(1)} custom-call(f32[1,128,128]{2,1,0:T(8,128)S(1)} %get-tuple-element.93), custom_call_target="InvertDiagBlocksLowerTriangular" | custom-call | tf_op jit(solution)/shard_map/jit(cholesky)/cholesky | solution.py:37
  287.4 11.9 %cholesky.243 = f32[128,128]{1,0:T(8,128)S(1)} custom-call(f32[128,128]{1,0:T(8,128)S(1)} %cholesky.581), custom_call_target="Cholesky" | custom-call | tf_op jit(solution)/shard_map/jit(cholesky)/cholesky | solution.py:37
  300.8 9.8 %custom-call.63 = f32[1,128,128]{1,2,0:T(8,128)S(1)} custom-call(f32[1,128,128]{2,1,0:T(8,128)S(1)} %get-tuple-element.90), custom_call_target="InvertDiagBlocksLowerTriangular" | custom-call | tf_op jit(solution)/shard_map/jit(cholesky)/cholesky | solution.py:37
  314.0 11.7 %cholesky.466 = f32[128,128]{1,0:T(8,128)S(1)} custom-call(f32[128,128]{1,0:T(8,128)S(1)} %cholesky.586), custom_call_target="Cholesky" | custom-call | tf_op jit(solution)/shard_map/jit(cholesky)/cholesky | solution.py:37
  327.0 9.8 %custom-call.64 = f32[1,128,128]{1,2,0:T(8,128)S(1)} custom-call(f32[1,128,128]{2,1,0:T(8,128)S(1)} %get-tuple-element.87), custom_call_target="InvertDiagBlocksLowerTriangular" | custom-call | tf_op jit(solution)/shard_map/jit(cholesky)/cholesky | solution.py:37
  340.3 11.9 %cholesky.485 = f32[128,128]{1,0:T(8,128)S(1)} custom-call(f32[128,128]{1,0:T(8,128)S(1)} %cholesky.591), custom_call_target="Cholesky" | custom-call | tf_op jit(solution)/shard_map/jit(cholesky)/cholesky | solution.py:37
  353.5 9.8 %custom-call.65 = f32[1,128,128]{1,2,0:T(8,128)S(1)} custom-call(f32[1,128,128]{2,1,0:T(8,128)S(1)} %get-tuple-element.84), custom_call_target="InvertDiagBlocksLowerTriangular" | custom-call | tf_op jit(solution)/shard_map/jit(cholesky)/cholesky | solution.py:37
  366.8 11.7 %cholesky.504 = f32[128,128]{1,0:T(8,128)S(1)} custom-call(f32[128,128]{1,0:T(8,128)S(1)} %cholesky.596), custom_call_target="Cholesky" | custom-call | tf_op jit(solution)/shard_map/jit(cholesky)/cholesky | solution.py:37
  379.9 10.3 %custom-call.66 = f32[1,128,128]{1,2,0:T(8,128)S(1)} custom-call(f32[1,128,128]{2,1,0:T(8,128)S(1)} %get-tuple-element.81), custom_call_target="InvertDiagBlocksLowerTriangular" | custom-call | tf_op jit(solution)/shard_map/jit(cholesky)/cholesky | solution.py:37
  393.5 11.7 %cholesky.524 = f32[128,128]{1,0:T(8,128)S(1)} custom-call(f32[128,128]{1,0:T(8,128)S(1)} %cholesky.601), custom_call_target="Cholesky" | custom-call | tf_op jit(solution)/shard_map/jit(cholesky)/cholesky | solution.py:37
  406.5 9.8 %custom-call.67 = f32[1,128,128]{1,2,0:T(8,128)S(1)} custom-call(f32[1,128,128]{2,1,0:T(8,128)S(1)} %get-tuple-element.78), custom_call_target="InvertDiagBlocksLowerTriangular" | custom-call | tf_op jit(solution)/shard_map/jit(cholesky)/cholesky | solution.py:37
  419.3 11.8 %cholesky.544 = f32[128,128]{1,0:T(8,128)S(1)} custom-call(f32[128,128]{1,0:T(8,128)S(1)} %cholesky.606), custom_call_target="Cholesky" | custom-call | tf_op jit(solution)/shard_map/jit(cholesky)/cholesky | solution.py:37
  432.4 9.8 %custom-call.68 = f32[1,128,128]{1,2,0:T(8,128)S(1)} custom-call(f32[1,128,128]{2,1,0:T(8,128)S(1)} %get-tuple-element.75), custom_call_target="InvertDiagBlocksLowerTriangular" | custom-call | tf_op jit(solution)/shard_map/jit(cholesky)/cholesky | solution.py:37
  444.8 11.7 %cholesky.562 = f32[128,128]{1,0:T(8,128)S(1)} custom-call(f32[128,128]{1,0:T(8,128)S(1)} %convolution_subtract_fusion.6), custom_call_target="Cholesky" | custom-call | tf_op jit(solution)/shard_map/jit(cholesky)/cholesky | solution.py:37
  463.5 6.6 %fusion.6 = (f32[1024,1024]{1,0:T(8,128)}, f32[1024,1024]{1,0:T(8,128)}) fusion(f32[1024,1024]{1,0:T(8,128)} %get-tuple-element.73, pred[]{:T(512)S(6)} %cholesky.576), kind=kLoop, calls=%fused_computation.13 | loop fusion | flops 4194304 | bytes 12582913 | tf_op jit(solution)/shard_map/triangular_solve | solution.py:38
  470.1 22.6 %while.14 = (s32[]{:T(128)}, f32[1024,1024]{1,0:T(8,128)}, s32[8,2]{0,1:T(2,128)S(1)}, f32[8,128,128]{2,1,0:T(8,128)S(1)}, s32[]{:T(128)}) while((s32[]{:T(128)}, f32[1024,1024]{1,0:T(8,128)}, s32[8,2]{0,1:T(2,128)S(1)}, f32[8,128,128]{2,1,0:T(8,128)S(1)}, s32[]{:T(128)}) %tuple.78), condition=%wide.while_cond, body=%wide.while_body.sunk | while | flops 2 | bytes 131181 | solution.py:38
  492.7 78.6 %custom-call.69 = f32[8,128,128]{1,2,0:T(8,128)S(1)} custom-call(f32[8,128,128]{2,1,0:T(8,128)S(1)} %get-tuple-element.45), custom_call_target="InvertDiagBlocksLowerTriangular" | custom-call | tf_op jit(solution)/shard_map/triangular_solve | solution.py:38
  (115 shorter events, 77.7 us)
Async XLA Ops:
  7.2 46.6 %copy-start = (f32[8,1024]{1,0:T(8,128)S(1)}, f32[8,1024]{1,0:T(8,128)}, u32[]{:S(2)}) copy-start(f32[8,1024]{1,0:T(8,128)} %param.10) | copy-start | bytes 98308
  7.2 240.2 %all-reduce.3.cloned.1.call-start = ((), (), s32[]{:S(2)}) async-start(), calls=%async_computation | async-start | bytes 8388608 | tf_op jit(solution)/shard_map/psum | solution.py:36
  7.9 7.2 %copy-start.2 = (bf16[4096]{0:T(1024)(128)(2,1)S(1)}, bf16[4096]{0:T(1024)(128)(2,1)}, u32[]{:S(2)}) copy-start(bf16[4096]{0:T(1024)(128)(2,1)} %param.8) | copy-start | bytes 24580
  60.4 0.7 copy-start.3
  257.6 1.9 copy-start.1
  583.9 0.6 copy-start.4
Sparse Core Ops, SparseCore 0:
  60.5 186.8 all-reduce.2
where the time goes:
time: 597 us; the launch traced here: 592 us
  other arithmetic  269 us (45%)
  blocking collectives  98.6 us (17%)
  waiting for transfers between devices  87.6 us (15%)
  matrix products  70.3 us (12%)
  local copies, waits for them, and re-layouts  45.3 us (8%)
  between operations  20.1 us (3%)
    another operation x30, other arithmetic, local(): factor = jnp.linalg.cholesky(total_gram)  173 us
    psum x1, blocking collectives, local(): lax.psum((gram_local, info_local), ('fibre', 'blk'))  98.6 us
    psum x1, waiting for transfers between devices, local(): lax.psum((gram_local, info_local), ('fibre', 'blk'))  87.6 us
    another operation x3, other arithmetic, local(): lax.linalg.triangular_solve(factor, total_info[:, None], left_side=True,...  85.2 us
    dot_general x4, matrix products, add_block(): lax.dot_general(row_piece, row_piece, (((0,), (0,)), ((), ())), preferred...  24.5 us
    another operation x14, matrix products, local(): factor = jnp.linalg.cholesky(total_gram)  22.7 us
    another operation x24, local copies, waits for them, and re-layouts  22.4 us
  transfers between devices with their start and end apart: 1, of which 1 were waited for; matrix products, arithmetic and copies ran while one was open for 0% of the time, Pallas kernels for 0%

commit v1 on v0

v1 whole, which is shorter than its diff:
```python
import jax, jax.numpy as jnp, numpy as np
from jax import lax
from jax.experimental import pallas as pl
from jax.experimental.pallas import tpu as pltpu
F32=jnp.float32
def bc(x,shape): return jnp.broadcast_to(x,shape)

def factor_block(T, n=16, W=256):
    out=[]
    sub=lax.broadcasted_iota(jnp.int32,(8,128),0)
    for p in range(n):
        V=T[p]
        C=[bc(V[:,8*p+c:8*p+c+1],(8,128)) for c in range(8)]
        Q={q:[bc(T[q][:,8*p+c:8*p+c+1],(8,128)) for c in range(8)] for q in range(p+1,n)}
        Vp=[V[:,128*w:128*w+128] for w in range(W//128)]
        rv=jnp.zeros((8,128),F32)
        rs=[];
        LQ={q:[] for q in Q}
        rows=[]
        for j in range(8):
            d=bc(C[j][j:j+1,:],(8,128))
            r=lax.rsqrt(d)
            L=C[j]*r
            Lm=jnp.where(sub>j,L,0.0) if j<7 else None
            rv=jnp.where(sub==j,r,rv)
            Rj=[bc(v[j:j+1,:],(8,128))*r for v in Vp]
            rows.append(Rj)
            if j<7:
                Vp=[v-Lm*rj for v,rj in zip(Vp,Rj)]
                Ls={k:bc(L[k:k+1,:],(8,128)) for k in range(j+1,8)}
                for k in range(j+1,8): C[k]=C[k]-L*Ls[k]
            for q in Q:
                Lq=Q[q][j]*r
                LQ[q].append(Lq)
                if j<7:
                    for k in range(j+1,8): Q[q][k]=Q[q][k]-Lq*Ls[k]
        out.append(jnp.concatenate([v*rv for v in Vp],axis=1))
        for q in Q:
            parts=[T[q][:,128*w:128*w+128] for w in range(W//128)]
            for j in range(8):
                parts=[a-LQ[q][j]*rj for a,rj in zip(parts,rows[j])]
            T[q]=jnp.concatenate(parts,axis=1)
    return out
BF=jnp.bfloat16
def split3(x):
    h=x.astype(BF); r=x-h.astype(F32); m=r.astype(BF); l=(r-m.astype(F32)).astype(BF)
    return h,m,l
def lhs6(x):
    h,m,l=split3(x); return jnp.concatenate([h,h,m,m,h,l],axis=1)
def rhs6(x):
    h,m,l=split3(x); return jnp.concatenate([h,m,h,m,l,h],axis=0)
def bidx(k,j): return 8*k-k*(k-1)//2+(j-k)
def chol_kernel(a_ref,b_ref,r_ref,y_ref,A,*,fac=factor_block):
    A[...]=a_ref[...]
    b=b_ref[...]
    ii=lax.broadcasted_iota(jnp.int32,(8,128),0); jj=lax.broadcasted_iota(jnp.int32,(8,128),1)
    def blk(k,j): return pl.ds(brow(bidx(k,j)),128)
    bl=[b[k:k+1,:] for k in range(8)]
    for k in range(8):
        o=brow(bidx(k,k))
        T=[jnp.concatenate([A[o+8*p:o+8*p+8,:],jnp.where(jj==ii+8*p,1.0,0.0).astype(F32)],axis=1) for p in range(16)]
        out=fac(T)
        for p in range(16): r_ref[128*k+8*p:128*k+8*p+8,128*k:128*k+128]=jnp.where(jj>=ii+8*p,out[p][:,:128],0.0)
        if k: r_ref[128*k:128*k+128,:128*k]=jnp.zeros((128,128*k),F32)
        Linv=jnp.concatenate([t[:,128:] for t in out],axis=0)
        bk=jnp.concatenate([bl[k],jnp.zeros((7,128),F32)],axis=0)
        yk=lax.dot_general(bk,Linv,(((1,),(1,)),((),())),precision=lax.Precision.HIGHEST,preferred_element_type=F32)
        y_ref[k:k+1,:]=yk[0:1,:]
        n=7-k
        if n==0: break
        row=jnp.concatenate([A[blk(k,j),:] for j in range(k+1,8)],axis=1)
        R=jnp.dot(lhs6(Linv),rhs6(row),preferred_element_type=F32)
        r_ref[128*k:128*k+128,128*(k+1):]=R
        X=jnp.concatenate([lhs6(R[:,128*i:128*i+128].T) for i in range(n)]+[lhs6(jnp.concatenate([yk,jnp.zeros((8,128),F32)],axis=0))],axis=0)
        Y=rhs6(R)
        for c in range(0,n,2):
            w=min(2,n-c)
            rows=128*(c+w)
            D=jnp.dot(jnp.concatenate([X[128*n:],X[:rows]],axis=0),Y[:,128*c:128*(c+w)],preferred_element_type=F32)
            for u in range(w):
                j=k+1+c+u
                bl[j]=bl[j]-D[0:1,128*u:128*u+128]
                for i in range(k+1,j+1):
                    z=16+128*(i-k-1)
                    A[blk(i,j),:]=A[blk(i,j),:]-D[z:z+128,128*u:128*u+128]
def chol_call(a,b,fac=factor_block):
    import functools
    return pl.pallas_call(functools.partial(chol_kernel,fac=fac),out_shape=(jax.ShapeDtypeStruct((1024,1024),F32),jax.ShapeDtypeStruct((8,128),F32)),
      scratch_shapes=[pltpu.VMEM((ROWS,128),F32)],compiler_params=pltpu.CompilerParams(vmem_limit_bytes=56*2**20))(a,b)
NS=1024; CAP=4096
CH=1024
def brow(i): return 128*i if i<12 else 128*i+256
INFO=1536
ROWS=4864
def gram_kernel(cnt_ref,pi_ref,x_ref,v_ref,pr_ref,g_ref):
    s=pl.program_id(0)
    x=x_ref[...]
    rowi=lax.broadcasted_iota(jnp.int32,(CH,NS),0)+s*CH
    xm=jnp.where(rowi<cnt_ref[0],x,jnp.zeros((),BF))
    xt=x.T
    v=jnp.broadcast_to(v_ref[...],(16,CH))
    def accum(first,xt,v,xm):
        lhs=jnp.concatenate([v,xt],axis=0)
        for c in range(4):
            D=lax.dot_general(lhs[:16+256*(c+1)],xm[:,256*c:256*c+256],(((1,),(0,)),((),())),preferred_element_type=F32)
            for u in range(2):
                j=2*c+u
                dv=D[0:1,128*u:128*u+128]
                if first: g_ref[INFO+j:INFO+j+1,:]=dv
                else: g_ref[INFO+j:INFO+j+1,:]=g_ref[INFO+j:INFO+j+1,:]+dv
                for i in range(j+1):
                    z=16+128*i; o=brow(bidx(i,j))
                    if first: g_ref[o:o+128,:]=D[z:z+128,128*u:128*u+128]
                    else: g_ref[o:o+128,:]=g_ref[o:o+128,:]+D[z:z+128,128*u:128*u+128]
    @pl.when(s==0)
    def _():
        accum(True,xt,v,xm)
        g_ref[INFO+8:INFO+256,:]=jnp.zeros((248,128),F32)
    @pl.when(s>0)
    def _(): accum(False,xt,v,xm)
    @pl.when(s==pl.num_programs(0)-1)
    def _():
        sub=lax.broadcasted_iota(jnp.int32,(8,128),0)
        pv=jnp.zeros((8,128),F32)
        for i in range(8): pv=jnp.where(sub==i,pi_ref[i],pv)
        pr=jnp.concatenate([pr_ref[...],pv],axis=1)
        h,m,l=split3(pr)
        h,m,l=[t.astype(F32) for t in (h,m,l)]
        z=jnp.zeros((80,NS+128),F32)
        a=jnp.concatenate([h,h,m,m,h,l,z],axis=0)
        b=jnp.concatenate([h,m,h,m,l,h,z],axis=0)[:,:NS].astype(BF)
        at=a.T.astype(BF)
        accum(False,at[:NS],at[NS:NS+16],b)
def gram_call(counts,prior_info,readings,values,prior_root):
    return pl.pallas_call(gram_kernel,grid=(CAP//CH,),
        in_specs=[pl.BlockSpec(memory_space=pltpu.SMEM),pl.BlockSpec(memory_space=pltpu.SMEM),
                  pl.BlockSpec((CH,NS),lambda s:(s,0)),pl.BlockSpec((1,CH),lambda s:(0,s)),
                  pl.BlockSpec((8,NS),lambda s:(0,0))],
        out_specs=pl.BlockSpec((ROWS,128),lambda s:(0,0)),
        out_shape=jax.ShapeDtypeStruct((ROWS,128),F32),
        compiler_params=pltpu.CompilerParams(vmem_limit_bytes=56*2**20))(counts,prior_info,readings,values.reshape(1,CAP),prior_root)
MESH=pl.DeviceIdType.MESH
CHUNKS=((0,1792),(1792,1536),(3328,1536))
DIMS=((0,1,2),(1,2,0),(2,0,1))
def comm_kernel(g_ref,a_ref,*scr):
    (r0,r1,r2,p0,p1,p2,ssem,rsem)=(scr[0:3],scr[3:6],scr[6:9],scr[9:12],scr[12:15],scr[15:18],scr[18],scr[19])
    f=lax.axis_index("fibre"); q=lax.axis_index("blk")
    core=f%2; co=(q//4,q%4,f//2)
    def peer(dim,d):
        c=list(co); c[dim]=(c[dim]+d)%4
        return (c[2]*2+core,c[0]*4+c[1])
    partner=(co[2]*2+(1-core),q)
    bar=pltpu.get_barrier_semaphore()
    pl.semaphore_signal(bar,inc=1,device_id=partner,device_id_type=MESH)
    for dim in range(3):
        for d in range(1,4):
            pl.semaphore_signal(bar,inc=1,device_id=peer(dim,d),device_id_type=MESH)
    pl.semaphore_wait(bar,10)
    cnt=[0]
    def send(src,dst,dev):
        i=cnt[0]; cnt[0]+=1
        c=pltpu.make_async_remote_copy(src_ref=src,dst_ref=dst,send_sem=ssem.at[i],recv_sem=rsem.at[i],device_id=dev,device_id_type=MESH)
        c.start(); return c
    al=lambda v: pl.multiple_of(v,8)
    H=[n//2 for _,n in CHUNKS]
    cs=[]
    for c,(b,n) in enumerate(CHUNKS):
        cs.append(send(g_ref.at[pl.ds(al(b+(1-core)*H[c]),H[c])],r0[c],partner))
    st=[]
    for c,(b,n) in enumerate(CHUNKS):
        cs[c].wait()
        p0[c][...]=g_ref[pl.ds(al(b+core*H[c]),H[c]),:]+r0[c][...]
        Q=H[c]//4; dim=DIMS[c][0]
        st.append([send(p0[c].at[pl.ds(al(((co[dim]+d)%4)*Q),Q)],r1[c].at[d-1],peer(dim,d)) for d in range(1,4)])
    st2=[]
    for c in range(3):
        for x in st[c]: x.wait()
        Q=H[c]//4; dim=DIMS[c][0]
        p1[c][...]=(p0[c][pl.ds(al(co[dim]*Q),Q),:]+r1[c][0])+(r1[c][1]+r1[c][2])
        Q2=Q//4; dim=DIMS[c][1]
        st2.append([send(p1[c].at[pl.ds(al(((co[dim]+d)%4)*Q2),Q2)],r2[c].at[d-1],peer(dim,d)) for d in range(1,4)])
    st3=[]
    for c in range(3):
        for x in st2[c]: x.wait()
        Q2=H[c]//16; dim=DIMS[c][1]; dz=DIMS[c][2]
        me=co[dz]
        p2[c][me]=(p1[c][pl.ds(al(co[dim]*Q2),Q2),:]+r2[c][0])+(r2[c][1]+r2[c][2])
        st3.append([send(p2[c].at[me],p2[c].at[me],peer(dz,d)) for d in range(1,4)])
    st4=[]
    def off(c,lvl):
        b=CHUNKS[c][0]; h=H[c]
        o=b+core*h
        if lvl>=1: o=o+co[DIMS[c][0]]*(h//4)
        if lvl>=2: o=o+co[DIMS[c][1]]*(h//16)
        return al(o)
    for c in range(3):
        for x in st3[c]: x.wait()
        n=H[c]//16; s=pl.ds(off(c,2),n)
        a_ref[s,:]=(p2[c][0]+p2[c][1])+(p2[c][2]+p2[c][3])
        st4.append([send(a_ref.at[s],a_ref.at[s],peer(DIMS[c][1],d)) for d in range(1,4)])
    st5=[]
    for c in range(3):
        for x in st4[c]: x.wait()
        s=pl.ds(off(c,1),H[c]//4)
        st5.append([send(a_ref.at[s],a_ref.at[s],peer(DIMS[c][0],d)) for d in range(1,4)])
    st6=[]
    for c in range(3):
        for x in st5[c]: x.wait()
        s=pl.ds(off(c,0),H[c])
        st6.append(send(a_ref.at[s],a_ref.at[s],partner))
    for x in st6: x.wait()
def comm_call(g):
    H=[n//2 for _,n in CHUNKS]
    V=lambda *s: pltpu.VMEM(s,F32)
    scr=[V(h,128) for h in H]+[V(3,h//4,128) for h in H]+[V(3,h//16,128) for h in H]+[V(h,128) for h in H]+[V(h//4,128) for h in H]+[V(4,h//16,128) for h in H]
    return pl.pallas_call(comm_kernel,out_shape=jax.ShapeDtypeStruct((ROWS,128),F32),
        in_specs=[pl.BlockSpec(memory_space=pltpu.VMEM)],out_specs=pl.BlockSpec(memory_space=pltpu.VMEM),
        scratch_shapes=scr+[pltpu.SemaphoreType.DMA((60,)),pltpu.SemaphoreType.DMA((60,))],
        compiler_params=pltpu.CompilerParams(collective_id=0,has_side_effects=True,vmem_limit_bytes=40*2**20))(g)
from jax.sharding import PartitionSpec as P
def local(readings,values,counts,prior_root,prior_info):
    g=gram_call(counts,prior_info,readings,values,prior_root)
    a=comm_call(g)
    R,y=chol_call(a,a[INFO:INFO+8])
    rows=lax.dynamic_slice_in_dim(R,lax.axis_index("blk")*64,64,0)
    return rows,y.reshape(1024)
def solution(mesh):
    placed=(P(("fibre","blk"),None),P(("fibre","blk")),P(("fibre","blk")),P(("fibre","blk"),None),P(("fibre","blk")))
    return jax.shard_map(local,mesh=mesh,in_specs=placed,out_specs=(P("blk",None),P()),check_vma=False)
```

time: 597 us -> 99.8 us (0.17)
  other arithmetic: 269 us -> 0 us
  blocking collectives: 98.6 us -> 0 us
  Pallas kernels: 0 us -> 92.1 us
  waiting for transfers between devices: 87.6 us -> 0 us
  matrix products: 70.3 us -> 0 us
  local copies, waits for them, and re-layouts: 45.3 us -> 6.16 us
  between operations: 20.1 us -> 1.3 us
    another operation x33 -> x0, other arithmetic: 258 us -> none  [the longest x30 173 us: local(): factor = jnp.linalg.cholesky(total_gram)]
    psum x1 -> x0, blocking collectives: 98.6 us -> none  [local(): lax.psum((gram_local, info_local), ('fibre', 'blk'))]
    pallas_call x0 -> x3, Pallas kernels: none -> 92.1 us  [the longest x1 41.5 us: chol_call(): pl.pallas_call(functools.partial(chol_kernel, fac=fac), out_shape=(jax.Sh...]
    psum x1 -> x0, waiting for transfers between devices: 87.6 us -> none  [local(): lax.psum((gram_local, info_local), ('fibre', 'blk'))]
    dot_general x10 -> x0, matrix products: 37.2 us -> none  [the longest x4 24.5 us: add_block(): lax.dot_general(row_piece, row_piece, (((0,), (0,)), ((), ())), preferred...]
    another operation x29 -> x0, matrix products: 33.2 us -> none  [the longest x14 22.7 us: local(): factor = jnp.linalg.cholesky(total_gram)]
    another operation x35 -> x0, local copies, waits for them, and re-layouts: 26 us -> none
    select_n x2 -> x0, other arithmetic: 7.23 us -> none  [the longest x1 7.23 us: local(): jnp.where(live_mask[:, None], readings, jnp.zeros((), readings.dtype))]
  transfers between devices with their start and end apart: 1 -> 0, of which waited for: 1 -> 0; matrix products, arithmetic and copies ran while one was open for 0% -> 0% of each run, Pallas kernels for 0% -> 0%
where the time goes in v1:
time: 99.8 us; the launch traced here: 99.6 us
  Pallas kernels  92.1 us (92%)
  local copies, waits for them, and re-layouts  6.16 us (6%)
  between operations  1.3 us (1%)
    pallas_call x1, Pallas kernels, chol_call(): pl.pallas_call(functools.partial(chol_kernel, fac=fac), out_shape=(jax.Sh...  41.5 us
    pallas_call x1, Pallas kernels, comm_call(): pl.pallas_call(comm_kernel, out_shape=jax.ShapeDtypeStruct((ROWS, 128), F...  38.2 us
    pallas_call x1, Pallas kernels, gram_call(): pl.pallas_call(gram_kernel, grid=(CAP // CH,), in_specs=[pl.BlockSpec(mem...  12.4 us
    unnamed x4, local copies, waits for them, and re-layouts  2.54 us

profile of v1, /device:TPU:1, one launch (start us, length us, event | category | flops | bytes accessed | tf_op | source)
XLA Modules:
  0.0 99.6 jit_solution(17560779327834174672)
XLA Ops:
  1.3 1.3 %reshape.10.v_ref = bf16[1,4096]{1,0:T(2,128)(2,1)} reshape(bf16[4096]{0:T(1024)(128)(2,1)} %param.6) | data formatting | bytes 16384 | tf_op jit(solution)/shard_map/reshape | solution.py:141
  2.6 12.4 %shard_map.68.g_ref = f32[4864,128]{1,0:T(8,128)} custom-call(s32[1]{0:T(128)S(6)} %copy.7.cnt_ref, f32[8]{0:T(128)} %pi_ref.1, bf16[4096,1024]{1,0:T(8,128)(2,1)} %x_ref.1, bf16[1,4096]{1,0:T(2,128)(2,1)} %reshape.10.v_ref, f32[8,1024]{1,0:T(8,128)} %pr_ref.1), custom_call_target="tpu_custom_call" | custom-call | tf_op jit(solution)/shard_map/pallas_call | solution.py:135
  15.0 0.0 copy-start.1
  15.0 1.7 %copy-done.1 = f32[4864,128]{1,0:T(8,128)S(1)} copy-done((f32[4864,128]{1,0:T(8,128)S(1)}, f32[4864,128]{1,0:T(8,128)}, u32[]{:S(2)}) %copy-start.1) | copy-done | bytes 2490392
  16.7 38.2 %shard_map.69.a_ref = f32[4864,128]{1,0:T(8,128)S(1)} custom-call(f32[4864,128]{1,0:T(8,128)S(1)} %copy-done.1), custom_call_target="tpu_custom_call" | custom-call | tf_op jit(solution)/shard_map/pallas_call | solution.py:216
  54.9 0.0 copy-start
  54.9 0.6 slice.3.b_ref
  55.5 0.8 copy-done
  56.4 41.5 %shard_map.70 = (f32[1024,1024]{1,0:T(8,128)}, f32[8,128]{1,0:T(8,128)}) custom-call(f32[4864,128]{1,0:T(8,128)} %copy-done, f32[8,128]{1,0:T(8,128)} %slice.3.b_ref), custom_call_target="tpu_custom_call" | custom-call | tf_op jit(solution)/shard_map/pallas_call | solution.py:88
  97.9 1.7 %constant_dynamic-slice_fusion = f32[64,1024]{1,0:T(8,128)} fusion(f32[1024,1024]{1,0:T(8,128)} %get-tuple-element.4, s32[]{:T(128)S(6)} %select_n.3), kind=kLoop, calls=%fused_computation | loop fusion | bytes 524292 | tf_op jit(solution)/shard_map/dynamic_slice | solution.py:225
Async XLA Ops:
  15.0 1.7 %copy-start.1 = (f32[4864,128]{1,0:T(8,128)S(1)}, f32[4864,128]{1,0:T(8,128)}, u32[]{:S(2)}) copy-start(f32[4864,128]{1,0:T(8,128)} %shard_map.68.g_ref) | copy-start | bytes 7471108
  54.9 1.5 %copy-start = (f32[4864,128]{1,0:T(8,128)}, f32[4864,128]{1,0:T(8,128)S(1)}, u32[]{:S(2)}) copy-start(f32[4864,128]{1,0:T(8,128)S(1)} %shard_map.69.a_ref) | copy-start | bytes 7471108

commit v2 on v1

--- a/solution.py
+++ b/solution.py
@@ -41,38 +41,175 @@
                 parts=[a-LQ[q][j]*rj for a,rj in zip(parts,rows[j])]
             T[q]=jnp.concatenate(parts,axis=1)
     return out
+def row(x,j): return bc(x[j:j+1,:],(8,128))
+def col(x,j): return bc(x[:,j:j+1],(8,128))
+def factor_inplace(T,slide=True):
+    T=list(T)
+    sub=lax.broadcasted_iota(jnp.int32,(8,128),0); lane=lax.broadcasted_iota(jnp.int32,(8,128),1)
+    R=[];I=[]
+    C=[col(T[0],c) for c in range(8)]
+    for p in range(16):
+        lo=8*p
+        inpan=(lane>=lo)&(lane<lo+8)
+        VA=T[p]
+        VX=jnp.where(inpan,jnp.where(lane==sub+lo,1.0,0.0),T[p])
+        Q={q:[col(T[q],lo+c) for c in range(8)] for q in range(p+1,16)}
+        Cn=[col(T[p+1],lo+8+c) for c in range(8)] if p<15 and slide else None
+        LQ={q:[] for q in Q}; RX=[]
+        oA=jnp.zeros((8,128),F32); oX=jnp.zeros((8,128),F32)
+        for j in (0,2,4,6):
+            a=row(C[j],j); b=row(C[j],j+1); c=row(C[j+1],j+1)
+            det=a*c-b*b
+            r1=lax.rsqrt(a); rd=lax.rsqrt(det); r2=r1*rd
+            W=a*C[j+1]-b*C[j]
+            s1=r1*r1; s2=r2*r2
+            L1=C[j]*r1; L2=W*r2
+            c1={k:row(C[j],k) for k in range(j+1,8)}
+            w2={k:row(W,k) for k in range(j+2,8)}
+            l1={k:c1[k]*r1 for k in c1}; l2={k:w2[k]*r2 for k in w2}
+            for k in range(j+2,8):
+                if k<j+4: C[k]=(C[k]-(C[j]*c1[k])*s1)-(W*w2[k])*s2
+                else: C[k]=(C[k]-L1*l1[k])-L2*l2[k]
+            g=a*r2
+            res=[]
+            for V in (VA,VX):
+                v0=row(V,j); v1=row(V,j+1)
+                res.append((v0*r1,(a*v1-b*v0)*r2))
+            (A0,A1),(X0,X1)=res
+            RX+= [X0,X1]
+            oA=jnp.where(sub==j,A0,jnp.where(sub==j+1,A1,oA))
+            oX=jnp.where(sub==j,X0,jnp.where(sub==j+1,X1,oX))
+            if j<6:
+                L1m=jnp.where(sub>j+1,L1,0.0); L2m=jnp.where(sub>j+1,L2,0.0)
+                VA=VA-L1m*A0-L2m*A1
+                VX=VX-L1m*X0-L2m*X1
+            for q in Q:
+                q0=Q[q][j]*r1
+                q1=(Q[q][j+1]-q0*l1[j+1])*g
+                LQ[q]+=[q0,q1]
+                for k in range(j+2,8): Q[q][k]=Q[q][k]-q0*l1[k]-q1*l2[k]
+        R.append(jnp.where(lane<lo+8,oA,oX)); I.append(oX)
+        if p<15:
+            for q in Q:
+                t=jnp.where(inpan,0.0,T[q])
+                for j in range(8): t=t-LQ[q][j]*RX[j]
+                T[q]=t
+            if slide:
+                for k in range(8):
+                    t=Cn[k]
+                    for j in range(8): t=t-LQ[p+1][j]*row(LQ[p+1][j],k)
+                    Cn[k]=t
+                C=Cn
+            else: C=[col(T[p+1],lo+8+c) for c in range(8)]
+    return R,I
 BF=jnp.bfloat16
 def split3(x):
+    h=x.astype(BF).astype(F32); r=x-h; m=r.astype(BF).astype(F32); l=r-m
+    return h,m,l
+def outer6(x):
+    h,m,l=split3(x)
+    a=jnp.concatenate([h,h,m,m,h,l],axis=0)
+    b=jnp.concatenate([h,m,h,m,l,h],axis=0).astype(BF)
+    return jnp.dot(a.T.astype(BF),b,preferred_element_type=F32)
+def factor_inplace2(T,G=3,order="mxu"):
+    T=list(T)
+    sub=lax.broadcasted_iota(jnp.int32,(8,128),0); lane=lax.broadcasted_iota(jnp.int32,(8,128),1)
+    R=[];I=[]
+    C=[col(T[0],c) for c in range(8)]
+    for p in range(16):
+        lo=8*p
+        inpan=(lane>=lo)&(lane<lo+8)
+        VA=T[p]
+        VX=jnp.where(inpan,jnp.where(lane==sub+lo,1.0,0.0),T[p])
+        near=range(p+1,min(p+1+G,16)); far=range(p+1+G,16)
+        Q={q:[col(T[q],lo+c) for c in range(8)] for q in near}
+        Cn=[col(T[p+1],lo+8+c) for c in range(8)] if p<15 else None
+        LQ={q:[] for q in near}; RX=[]
+        oA=jnp.zeros((8,128),F32); oX=jnp.zeros((8,128),F32)
+        for j in (0,2,4,6):
+            a=row(C[j],j); b=row(C[j],j+1); c=row(C[j+1],j+1)
+            det=a*c-b*b
+            r1=lax.rsqrt(a); rd=lax.rsqrt(det); r2=r1*rd
+            W=a*C[j+1]-b*C[j]
+            s1=r1*r1; s2=r2*r2
+            L1=C[j]*r1; L2=W*r2
+            c1={k:row(C[j],k) for k in range(j+1,8)}
+            w2={k:row(W,k) for k in range(j+2,8)}
+            l1={k:c1[k]*r1 for k in c1}; l2={k:w2[k]*r2 for k in w2}
+            for k in range(j+2,8):
+                if k<j+4: C[k]=(C[k]-(C[j]*c1[k])*s1)-(W*w2[k])*s2
+                else: C[k]=(C[k]-L1*l1[k])-L2*l2[k]
+            g=a*r2
+            res=[]
+            for V in (VA,VX):
+                v0=row(V,j); v1=row(V,j+1)
+                res.append((v0*r1,(a*v1-b*v0)*r2))
+            (A0,A1),(X0,X1)=res
+            RX+= [X0,X1]
+            oA=jnp.where(sub==j,A0,jnp.where(sub==j+1,A1,oA))
+            oX=jnp.where(sub==j,X0,jnp.where(sub==j+1,X1,oX))
+            if j<6:
+                L1m=jnp.where(sub>j+1,L1,0.0); L2m=jnp.where(sub>j+1,L2,0.0)
+                VA=VA-L1m*A0-L2m*A1
+                VX=VX-L1m*X0-L2m*X1
+            for q in Q:
+                q0=Q[q][j]*r1
+                q1=(Q[q][j+1]-q0*l1[j+1])*g
+                LQ[q]+=[q0,q1]
+                for k in range(j+2,8): Q[q][k]=Q[q][k]-q0*l1[k]-q1*l2[k]
+        R.append(jnp.where(lane<lo+8,oA,oX)); I.append(oX)
+        if p<15:
+            if len(far):
+                D=outer6(oX)
+            for q in near:
+                t=jnp.where(inpan,0.0,T[q])
+                for j in range(8): t=t-LQ[q][j]*RX[j]
+                T[q]=t
+            for k in range(8):
+                t=Cn[k]
+                for j in range(8): t=t-LQ[p+1][j]*row(LQ[p+1][j],k)
+                Cn[k]=t
+            C=Cn
+            for q in far:
+                T[q]=jnp.where(inpan,0.0,T[q])-D[8*q:8*q+8,:]
+    return R,I
+def split3b(x):
     h=x.astype(BF); r=x-h.astype(F32); m=r.astype(BF); l=(r-m.astype(F32)).astype(BF)
     return h,m,l
 def lhs6(x):
-    h,m,l=split3(x); return jnp.concatenate([h,h,m,m,h,l],axis=1)
+    h,m,l=split3b(x); return jnp.concatenate([h,h,m,m,h,l],axis=1)
 def rhs6(x):
-    h,m,l=split3(x); return jnp.concatenate([h,m,h,m,l,h],axis=0)
+    h,m,l=split3b(x); return jnp.concatenate([h,m,h,m,l,h],axis=0)
 def bidx(k,j): return 8*k-k*(k-1)//2+(j-k)
-def chol_kernel(a_ref,b_ref,r_ref,y_ref,A,*,fac=factor_block):
-    A[...]=a_ref[...]
-    b=b_ref[...]
+def blk(k,j): return pl.ds(brow(bidx(k,j)),128)
+def chol_kernel(a_ref,r_ref,y_ref,A,Rs,Li):
     ii=lax.broadcasted_iota(jnp.int32,(8,128),0); jj=lax.broadcasted_iota(jnp.int32,(8,128),1)
-    def blk(k,j): return pl.ds(brow(bidx(k,j)),128)
-    bl=[b[k:k+1,:] for k in range(8)]
+    big=(128,128)
+    eye=lax.broadcasted_iota(jnp.int32,big,0)==lax.broadcasted_iota(jnp.int32,big,1)
+    dg=[jnp.sum(jnp.where(eye,a_ref[blk(k,k),:],0.0),axis=0,keepdims=True) for k in range(8)]
+    dr=[lax.rsqrt(d) for d in dg]
+    for k in range(8):
+        dc=bc(dr[k],big).T
+        for j in range(k,8): A[blk(k,j),:]=a_ref[blk(k,j),:]*dc*dr[j]
+    bl=[a_ref[INFO+k:INFO+k+1,:]*dr[k] for k in range(8)]
     for k in range(8):
         o=brow(bidx(k,k))
-        T=[jnp.concatenate([A[o+8*p:o+8*p+8,:],jnp.where(jj==ii+8*p,1.0,0.0).astype(F32)],axis=1) for p in range(16)]
-        out=fac(T)
-        for p in range(16): r_ref[128*k+8*p:128*k+8*p+8,128*k:128*k+128]=jnp.where(jj>=ii+8*p,out[p][:,:128],0.0)
-        if k: r_ref[128*k:128*k+128,:128*k]=jnp.zeros((128,128*k),F32)
-        Linv=jnp.concatenate([t[:,128:] for t in out],axis=0)
+        R,I=factor_inplace2([A[o+8*p:o+8*p+8,:] for p in range(16)])
+        for p in range(16):
+            Rs[128*k+8*p:128*k+8*p+8,128*k:128*k+128]=jnp.where(jj>=ii+8*p,R[p],0.0)
+            Li[8*p:8*p+8,:]=jnp.where(jj<8*p+8,I[p],0.0)
+        if k: Rs[128*k:128*k+128,:128*k]=jnp.zeros((128,128*k),F32)
+        Linv=Li[...]
         bk=jnp.concatenate([bl[k],jnp.zeros((7,128),F32)],axis=0)
         yk=lax.dot_general(bk,Linv,(((1,),(1,)),((),())),precision=lax.Precision.HIGHEST,preferred_element_type=F32)
         y_ref[k:k+1,:]=yk[0:1,:]
         n=7-k
         if n==0: break
-        row=jnp.concatenate([A[blk(k,j),:] for j in range(k+1,8)],axis=1)
-        R=jnp.dot(lhs6(Linv),rhs6(row),preferred_element_type=F32)
-        r_ref[128*k:128*k+128,128*(k+1):]=R
-        X=jnp.concatenate([lhs6(R[:,128*i:128*i+128].T) for i in range(n)]+[lhs6(jnp.concatenate([yk,jnp.zeros((8,128),F32)],axis=0))],axis=0)
-        Y=rhs6(R)
+        row_=jnp.concatenate([A[blk(k,j),:] for j in range(k+1,8)],axis=1)
+        Rk=jnp.dot(lhs6(Linv),rhs6(row_),preferred_element_type=F32)
+        Rs[128*k:128*k+128,128*(k+1):]=Rk
+        X=jnp.concatenate([lhs6(Rk[:,128*i:128*i+128].T) for i in range(n)]+[lhs6(jnp.concatenate([yk,jnp.zeros((8,128),F32)],axis=0))],axis=0)
+        Y=rhs6(Rk)
         for c in range(0,n,2):
             w=min(2,n-c)
             rows=128*(c+w)
@@ -83,10 +220,14 @@
                 for i in range(k+1,j+1):
                     z=16+128*(i-k-1)
                     A[blk(i,j),:]=A[blk(i,j),:]-D[z:z+128,128*u:128*u+128]
-def chol_call(a,b,fac=factor_block):
-    import functools
-    return pl.pallas_call(functools.partial(chol_kernel,fac=fac),out_shape=(jax.ShapeDtypeStruct((1024,1024),F32),jax.ShapeDtypeStruct((8,128),F32)),
-      scratch_shapes=[pltpu.VMEM((ROWS,128),F32)],compiler_params=pltpu.CompilerParams(vmem_limit_bytes=56*2**20))(a,b)
+    s=pl.multiple_of(rowstart(),64)
+    for j in range(8):
+        r_ref[:,128*j:128*j+128]=Rs[pl.ds(s,64),128*j:128*j+128]*(dg[j]*dr[j])
+def rowstart(): return lax.axis_index("blk")*64
+def chol_call(a):
+    return pl.pallas_call(chol_kernel,out_shape=(jax.ShapeDtypeStruct((64,1024),F32),jax.ShapeDtypeStruct((8,128),F32)),
+      in_specs=[pl.BlockSpec(memory_space=pltpu.VMEM)],
+      scratch_shapes=[pltpu.VMEM((ROWS,128),F32),pltpu.VMEM((1024,1024),F32),pltpu.VMEM((128,128),F32)],compiler_params=pltpu.CompilerParams(vmem_limit_bytes=32*2**20))(a)
 NS=1024; CAP=4096
 CH=1024
 def brow(i): return 128*i if i<12 else 128*i+256
@@ -98,7 +239,8 @@
     rowi=lax.broadcasted_iota(jnp.int32,(CH,NS),0)+s*CH
     xm=jnp.where(rowi<cnt_ref[0],x,jnp.zeros((),BF))
     xt=x.T
-    v=jnp.broadcast_to(v_ref[...],(16,CH))
+    vf=v_ref[pl.ds(pl.multiple_of(s*(CH//128),8),CH//128),:].astype(F32)
+    v=jnp.broadcast_to(jnp.concatenate([vf[i:i+1,:] for i in range(CH//128)],axis=1),(16,CH)).astype(BF)
     def accum(first,xt,v,xm):
         lhs=jnp.concatenate([v,xt],axis=0)
         for c in range(4):
@@ -124,7 +266,7 @@
         pv=jnp.zeros((8,128),F32)
         for i in range(8): pv=jnp.where(sub==i,pi_ref[i],pv)
         pr=jnp.concatenate([pr_ref[...],pv],axis=1)
-        h,m,l=split3(pr)
+        h,m,l=split3b(pr)
         h,m,l=[t.astype(F32) for t in (h,m,l)]
         z=jnp.zeros((80,NS+128),F32)
         a=jnp.concatenate([h,h,m,m,h,l,z],axis=0)
@@ -134,11 +276,11 @@
 def gram_call(counts,prior_info,readings,values,prior_root):
     return pl.pallas_call(gram_kernel,grid=(CAP//CH,),
         in_specs=[pl.BlockSpec(memory_space=pltpu.SMEM),pl.BlockSpec(memory_space=pltpu.SMEM),
-                  pl.BlockSpec((CH,NS),lambda s:(s,0)),pl.BlockSpec((1,CH),lambda s:(0,s)),
+                  pl.BlockSpec((CH,NS),lambda s:(s,0)),pl.BlockSpec((CAP//128,128),lambda s:(0,0)),
                   pl.BlockSpec((8,NS),lambda s:(0,0))],
-        out_specs=pl.BlockSpec((ROWS,128),lambda s:(0,0)),
+        out_specs=pl.BlockSpec(memory_space=pltpu.VMEM),
         out_shape=jax.ShapeDtypeStruct((ROWS,128),F32),
-        compiler_params=pltpu.CompilerParams(vmem_limit_bytes=56*2**20))(counts,prior_info,readings,values.reshape(1,CAP),prior_root)
+        compiler_params=pltpu.CompilerParams(vmem_limit_bytes=56*2**20))(counts,prior_info,readings,values.reshape(CAP//128,128),prior_root)
 MESH=pl.DeviceIdType.MESH
 CHUNKS=((0,1792),(1792,1536),(3328,1536))
 DIMS=((0,1,2),(1,2,0),(2,0,1))
@@ -221,8 +363,7 @@
 def local(readings,values,counts,prior_root,prior_info):
     g=gram_call(counts,prior_info,readings,values,prior_root)
     a=comm_call(g)
-    R,y=chol_call(a,a[INFO:INFO+8])
-    rows=lax.dynamic_slice_in_dim(R,lax.axis_index("blk")*64,64,0)
+    rows,y=chol_call(a)
     return rows,y.reshape(1024)
 def solution(mesh):
     placed=(P(("fibre","blk"),None),P(("fibre","blk")),P(("fibre","blk")),P(("fibre","blk"),None),P(("fibre","blk")))

time: 99.8 us -> 81.1 us (0.81)
  Pallas kernels: 92.1 us -> 78 us
  local copies, waits for them, and re-layouts: 6.16 us -> 1.7 us
    pallas_call x1, Pallas kernels: 41.5 us -> 27.4 us  [chol_call(): pl.pallas_call(chol_kernel, out_shape=(jax.ShapeDtypeStruct((64, 1024), F...]
    dynamic_slice x1 -> x0, local copies, waits for them, and re-layouts: 1.67 us -> none  [local(): rows = lax.dynamic_slice_in_dim(R, lax.axis_index('blk') * 64, 64, 0)]
    reshape x1 -> x0, local copies, waits for them, and re-layouts: 1.31 us -> none  [gram_call(): values.reshape(1, CAP)]
    unnamed x4 -> x2, local copies, waits for them, and re-layouts: 2.54 us -> 1.7 us
where the time goes in v2:
time: 81.1 us; the launch traced here: 81 us
  Pallas kernels  78 us (96%)
  local copies, waits for them, and re-layouts  1.7 us (2%)
  between operations  1.29 us (2%)
    pallas_call x1, Pallas kernels, comm_call(): pl.pallas_call(comm_kernel, out_shape=jax.ShapeDtypeStruct((ROWS, 128), F...  38.2 us
    pallas_call x1, Pallas kernels, chol_call(): pl.pallas_call(chol_kernel, out_shape=(jax.ShapeDtypeStruct((64, 1024), F...  27.4 us
    pallas_call x1, Pallas kernels, gram_call(): pl.pallas_call(gram_kernel, grid=(CAP // CH,), in_specs=[pl.BlockSpec(mem...  12.4 us
    unnamed x2, local copies, waits for them, and re-layouts  1.7 us

profile of v2, /device:TPU:1, one launch (start us, length us, event | category | flops | bytes accessed | tf_op | source)
XLA Modules:
  0.0 81.0 jit_solution(6628339817093779017)
XLA Ops:
  1.3 12.4 %shard_map.68.g_ref = f32[4864,128]{1,0:T(8,128)} custom-call(s32[1]{0:T(128)S(6)} %copy.7.cnt_ref, f32[8]{0:T(128)} %pi_ref.1, bf16[4096,1024]{1,0:T(8,128)(2,1)} %x_ref.1, bf16[32,128]{1,0:T(8,128)(2,1)} %bitcast.2, f32[8,1024]{1,0:T(8,128)} %pr_ref.1), custom_call_target="tpu_custom_call" | custom-call | tf_op jit(solution)/shard_map/pallas_call | solution.py:277
  13.7 0.0 copy-start
  13.7 1.7 %copy-done = f32[4864,128]{1,0:T(8,128)S(1)} copy-done((f32[4864,128]{1,0:T(8,128)S(1)}, f32[4864,128]{1,0:T(8,128)}, u32[]{:S(2)}) %copy-start) | copy-done | bytes 2490392
  15.4 38.2 %shard_map.69.a_ref = f32[4864,128]{1,0:T(8,128)S(1)} custom-call(f32[4864,128]{1,0:T(8,128)S(1)} %copy-done), custom_call_target="tpu_custom_call" | custom-call | tf_op jit(solution)/shard_map/pallas_call | solution.py:358
  53.6 27.4 %shard_map.70 = (f32[64,1024]{1,0:T(8,128)}, f32[8,128]{1,0:T(8,128)}) custom-call(f32[4864,128]{1,0:T(8,128)S(1)} %shard_map.69.a_ref), custom_call_target="tpu_custom_call" | custom-call | tf_op jit(solution)/shard_map/pallas_call | solution.py:228
Async XLA Ops:
  13.7 1.7 %copy-start = (f32[4864,128]{1,0:T(8,128)S(1)}, f32[4864,128]{1,0:T(8,128)}, u32[]{:S(2)}) copy-start(f32[4864,128]{1,0:T(8,128)} %shard_map.68.g_ref) | copy-start | bytes 7471108

commit v3 on v2

v3 whole, which is shorter than its diff:
```python
import jax, jax.numpy as jnp, numpy as np
from jax import lax
from jax.experimental import pallas as pl
from jax.experimental.pallas import tpu as pltpu
F32=jnp.float32
def bc(x,shape): return jnp.broadcast_to(x,shape)

def factor_block(T, n=16, W=256):
    out=[]
    sub=lax.broadcasted_iota(jnp.int32,(8,128),0)
    for p in range(n):
        V=T[p]
        C=[bc(V[:,8*p+c:8*p+c+1],(8,128)) for c in range(8)]
        Q={q:[bc(T[q][:,8*p+c:8*p+c+1],(8,128)) for c in range(8)] for q in range(p+1,n)}
        Vp=[V[:,128*w:128*w+128] for w in range(W//128)]
        rv=jnp.zeros((8,128),F32)
        rs=[];
        LQ={q:[] for q in Q}
        rows=[]
        for j in range(8):
            d=bc(C[j][j:j+1,:],(8,128))
            r=lax.rsqrt(d)
            L=C[j]*r
            Lm=jnp.where(sub>j,L,0.0) if j<7 else None
            rv=jnp.where(sub==j,r,rv)
            Rj=[bc(v[j:j+1,:],(8,128))*r for v in Vp]
            rows.append(Rj)
            if j<7:
                Vp=[v-Lm*rj for v,rj in zip(Vp,Rj)]
                Ls={k:bc(L[k:k+1,:],(8,128)) for k in range(j+1,8)}
                for k in range(j+1,8): C[k]=C[k]-L*Ls[k]
            for q in Q:
                Lq=Q[q][j]*r
                LQ[q].append(Lq)
                if j<7:
                    for k in range(j+1,8): Q[q][k]=Q[q][k]-Lq*Ls[k]
        out.append(jnp.concatenate([v*rv for v in Vp],axis=1))
        for q in Q:
            parts=[T[q][:,128*w:128*w+128] for w in range(W//128)]
            for j in range(8):
                parts=[a-LQ[q][j]*rj for a,rj in zip(parts,rows[j])]
            T[q]=jnp.concatenate(parts,axis=1)
    return out
def row(x,j): return bc(x[j:j+1,:],(8,128))
def col(x,j): return bc(x[:,j:j+1],(8,128))
def factor_inplace(T,slide=True):
    T=list(T)
    sub=lax.broadcasted_iota(jnp.int32,(8,128),0); lane=lax.broadcasted_iota(jnp.int32,(8,128),1)
    R=[];I=[]
    C=[col(T[0],c) for c in range(8)]
    for p in range(16):
        lo=8*p
        inpan=(lane>=lo)&(lane<lo+8)
        VA=T[p]
        VX=jnp.where(inpan,jnp.where(lane==sub+lo,1.0,0.0),T[p])
        Q={q:[col(T[q],lo+c) for c in range(8)] for q in range(p+1,16)}
        Cn=[col(T[p+1],lo+8+c) for c in range(8)] if p<15 and slide else None
        LQ={q:[] for q in Q}; RX=[]
        oA=jnp.zeros((8,128),F32); oX=jnp.zeros((8,128),F32)
        for j in (0,2,4,6):
            a=row(C[j],j); b=row(C[j],j+1); c=row(C[j+1],j+1)
            det=a*c-b*b
            r1=lax.rsqrt(a); rd=lax.rsqrt(det); r2=r1*rd
            W=a*C[j+1]-b*C[j]
            s1=r1*r1; s2=r2*r2
            L1=C[j]*r1; L2=W*r2
            c1={k:row(C[j],k) for k in range(j+1,8)}
            w2={k:row(W,k) for k in range(j+2,8)}
            l1={k:c1[k]*r1 for k in c1}; l2={k:w2[k]*r2 for k in w2}
            for k in range(j+2,8):
                if k<j+4: C[k]=(C[k]-(C[j]*c1[k])*s1)-(W*w2[k])*s2
                else: C[k]=(C[k]-L1*l1[k])-L2*l2[k]
            g=a*r2
            res=[]
            for V in (VA,VX):
                v0=row(V,j); v1=row(V,j+1)
                res.append((v0*r1,(a*v1-b*v0)*r2))
            (A0,A1),(X0,X1)=res
            RX+= [X0,X1]
            oA=jnp.where(sub==j,A0,jnp.where(sub==j+1,A1,oA))
            oX=jnp.where(sub==j,X0,jnp.where(sub==j+1,X1,oX))
            if j<6:
                L1m=jnp.where(sub>j+1,L1,0.0); L2m=jnp.where(sub>j+1,L2,0.0)
                VA=VA-L1m*A0-L2m*A1
                VX=VX-L1m*X0-L2m*X1
            for q in Q:
                q0=Q[q][j]*r1
                q1=(Q[q][j+1]-q0*l1[j+1])*g
                LQ[q]+=[q0,q1]
                for k in range(j+2,8): Q[q][k]=Q[q][k]-q0*l1[k]-q1*l2[k]
        R.append(jnp.where(lane<lo+8,oA,oX)); I.append(oX)
        if p<15:
            for q in Q:
                t=jnp.where(inpan,0.0,T[q])
                for j in range(8): t=t-LQ[q][j]*RX[j]
                T[q]=t
            if slide:
                for k in range(8):
                    t=Cn[k]
                    for j in range(8): t=t-LQ[p+1][j]*row(LQ[p+1][j],k)
                    Cn[k]=t
                C=Cn
            else: C=[col(T[p+1],lo+8+c) for c in range(8)]
    return R,I
BF=jnp.bfloat16
def split3(x):
    h=x.astype(BF).astype(F32); r=x-h; m=r.astype(BF).astype(F32); l=r-m
    return h,m,l
def outer6(x):
    h,m,l=split3(x)
    a=jnp.concatenate([h,h,m,m,h,l],axis=0)
    b=jnp.concatenate([h,m,h,m,l,h],axis=0).astype(BF)
    return jnp.dot(a.T.astype(BF),b,preferred_element_type=F32)
def factor_inplace2(T,G=3,order="mxu"):
    T=list(T)
    sub=lax.broadcasted_iota(jnp.int32,(8,128),0); lane=lax.broadcasted_iota(jnp.int32,(8,128),1)
    R=[];I=[]
    C=[col(T[0],c) for c in range(8)]
    for p in range(16):
        lo=8*p
        inpan=(lane>=lo)&(lane<lo+8)
        VA=T[p]
        VX=jnp.where(inpan,jnp.where(lane==sub+lo,1.0,0.0),T[p])
        near=range(p+1,min(p+1+G,16)); far=range(p+1+G,16)
        Q={q:[col(T[q],lo+c) for c in range(8)] for q in near}
        Cn=[col(T[p+1],lo+8+c) for c in range(8)] if p<15 else None
        LQ={q:[] for q in near}; RX=[]
        oA=jnp.zeros((8,128),F32); oX=jnp.zeros((8,128),F32)
        for j in (0,2,4,6):
            a=row(C[j],j); b=row(C[j],j+1); c=row(C[j+1],j+1)
            det=a*c-b*b
            r1=lax.rsqrt(a); rd=lax.rsqrt(det); r2=r1*rd
            W=a*C[j+1]-b*C[j]
            s1=r1*r1; s2=r2*r2
            L1=C[j]*r1; L2=W*r2
            c1={k:row(C[j],k) for k in range(j+1,8)}
            w2={k:row(W,k) for k in range(j+2,8)}
            l1={k:c1[k]*r1 for k in c1}; l2={k:w2[k]*r2 for k in w2}
            for k in range(j+2,8):
                if k<j+4: C[k]=(C[k]-(C[j]*c1[k])*s1)-(W*w2[k])*s2
                else: C[k]=(C[k]-L1*l1[k])-L2*l2[k]
            g=a*r2
            res=[]
            for V in (VA,VX):
                v0=row(V,j); v1=row(V,j+1)
                res.append((v0*r1,(a*v1-b*v0)*r2))
            (A0,A1),(X0,X1)=res
            RX+= [X0,X1]
            oA=jnp.where(sub==j,A0,jnp.where(sub==j+1,A1,oA))
            oX=jnp.where(sub==j,X0,jnp.where(sub==j+1,X1,oX))
            if j<6:
                L1m=jnp.where(sub>j+1,L1,0.0); L2m=jnp.where(sub>j+1,L2,0.0)
                VA=VA-L1m*A0-L2m*A1
                VX=VX-L1m*X0-L2m*X1
            for q in Q:
                q0=Q[q][j]*r1
                q1=(Q[q][j+1]-q0*l1[j+1])*g
                LQ[q]+=[q0,q1]
                for k in range(j+2,8): Q[q][k]=Q[q][k]-q0*l1[k]-q1*l2[k]
        R.append(jnp.where(lane<lo+8,oA,oX)); I.append(oX)
        if p<15:
            if len(far):
                D=outer6(oX)
            for q in near:
                t=jnp.where(inpan,0.0,T[q])
                for j in range(8): t=t-LQ[q][j]*RX[j]
                T[q]=t
            for k in range(8):
                t=Cn[k]
                for j in range(8): t=t-LQ[p+1][j]*row(LQ[p+1][j],k)
                Cn[k]=t
            C=Cn
            for q in far:
                T[q]=jnp.where(inpan,0.0,T[q])-D[8*q:8*q+8,:]
    return R,I
MESH=pl.DeviceIdType.MESH
NS=1024; CAP=4096; CH=1024; STEPS=CAP//CH; ROWS=4608
PIECES=((0,512,(0,1,2)),(512,512,(1,2,0)),(1024,512,(2,0,1)),(1536,1024,(0,1,2)),(2560,1024,(1,2,0)),(3584,1024,(2,0,1)))
HALF=[n//2 for _,n,_ in PIECES]
def split3b(x):
    h=x.astype(BF); r=x-h.astype(F32); m=r.astype(BF); l=(r-m.astype(F32)).astype(BF)
    return h,m,l
def lhs6(x):
    h,m,l=split3b(x); return jnp.concatenate([h,h,m,m,h,l],axis=1)
def rhs6(x):
    h,m,l=split3b(x); return jnp.concatenate([h,m,h,m,l,h],axis=0)
def brow(k,j): return 128*(8*k-k*(k-1)//2+(j-k))
def blk(k,j): return pl.ds(brow(k,j),128)

def gram_part(s,cnt_ref,pi_ref,x_ref,v_ref,pr_ref,g,info):
    x=x_ref[...]
    rowi=lax.broadcasted_iota(jnp.int32,(CH,NS),0)+s*CH
    xm=jnp.where(rowi<cnt_ref[0],x,jnp.zeros((),BF))
    xt=x.T
    vf=v_ref[pl.ds(pl.multiple_of(s*(CH//128),8),CH//128),:].astype(F32)
    v=jnp.broadcast_to(jnp.concatenate([vf[i:i+1,:] for i in range(CH//128)],axis=1),(16,CH)).astype(BF)
    def accum(first,xt,v,xm):
        lhs=jnp.concatenate([v,xt],axis=0)
        for c in range(4):
            D=jnp.dot(lhs[:16+256*(c+1)],xm[:,256*c:256*c+256],preferred_element_type=F32)
            for u in range(2):
                j=2*c+u
                dv=D[0:1,128*u:128*u+128]
                info[j:j+1,:]=dv if first else info[j:j+1,:]+dv
                for i in range(j+1):
                    z=16+128*i; d=D[z:z+128,128*u:128*u+128]
                    g[blk(i,j),:]=d if first else g[blk(i,j),:]+d
    @pl.when(s==0)
    def _(): accum(True,xt,v,xm)
    @pl.when(s>0)
    def _(): accum(False,xt,v,xm)
    @pl.when(s==STEPS-1)
    def _():
        sub=lax.broadcasted_iota(jnp.int32,(8,128),0)
        pv=jnp.zeros((8,128),F32)
        for i in range(8): pv=jnp.where(sub==i,pi_ref[i],pv)
        h,m,l=split3(jnp.concatenate([pr_ref[...],pv],axis=1))
        z=jnp.zeros((80,NS+128),F32)
        a=jnp.concatenate([h,h,m,m,h,l,z],axis=0)
        b=jnp.concatenate([h,m,h,m,l,h,z],axis=0)[:,:NS].astype(BF)
        at=a.T.astype(BF)
        accum(False,at[:NS],at[NS:NS+16],b)
        eye=lax.broadcasted_iota(jnp.int32,(128,128),0)==lax.broadcasted_iota(jnp.int32,(128,128),1)
        lane=lax.broadcasted_iota(jnp.int32,(1,128),1)
        for k in range(8):
            dg=jnp.sum(jnp.where(eye,g[blk(k,k),:],0.0),axis=0,keepdims=True)
            for base,r in ((64,info[k:k+1,:]),(80,dg)):
                rr=pltpu.roll(jnp.broadcast_to(r,(8,128)),64,1)[0:1,:]
                g[base+2*k:base+2*k+1,:]=jnp.where(lane<64,r,g[base+2*k:base+2*k+1,:])
                g[base+2*k+1:base+2*k+2,:]=jnp.where(lane<64,rr,g[base+2*k+1:base+2*k+2,:])

class Comm:
    def __init__(self,g,a,r0,r1,r2,p0,p1,p2,ssem,rsem):
        self.__dict__.update(g=g,a=a,r0=r0,r1=r1,r2=r2,p0=p0,p1=p1,p2=p2,ssem=ssem,rsem=rsem)
        f=lax.axis_index("fibre"); q=lax.axis_index("blk")
        self.core=f%2; self.co=(q//4,q%4,f//2); self.q=q; self.n=0; self.fly={}
        self.partner=(self.co[2]*2+(1-self.core),q)
    def peer(self,dim,d):
        c=list(self.co); c[dim]=(c[dim]+d)%4
        return (c[2]*2+self.core,c[0]*4+c[1])
    def greet(self):
        bar=pltpu.get_barrier_semaphore()
        pl.semaphore_signal(bar,inc=1,device_id=self.partner,device_id_type=MESH)
        for dim in range(3):
            for d in range(1,4):
                pl.semaphore_signal(bar,inc=1,device_id=self.peer(dim,d),device_id_type=MESH)
    def met(self): pl.semaphore_wait(pltpu.get_barrier_semaphore(),10)
    def send(self,src,dst,dev):
        i=self.n; self.n+=1
        c=pltpu.make_async_remote_copy(src_ref=src,dst_ref=dst,send_sem=self.ssem.at[i],recv_sem=self.rsem.at[i],device_id=dev,device_id_type=MESH)
        c.start(); return c
    def off(self,c,lvl):
        b,_,dims=PIECES[c]; h=HALF[c]
        o=b+self.core*h
        if lvl>=1: o=o+self.co[dims[0]]*(h//4)
        if lvl>=2: o=o+self.co[dims[1]]*(h//16)
        return pl.multiple_of(o,8)
    def step(self,n,cs):
        al=lambda v: pl.multiple_of(v,8)
        for c in cs:
            b,_,dims=PIECES[c]; h=HALF[c]; h4=h//4; h16=h//16
            for x in self.fly.pop(c,()): x.wait()
            core,co=self.core,self.co
            if n==0:
                out=[self.send(self.g.at[pl.ds(al(b+(1-core)*h),h)],self.r0[c],self.partner)]
            elif n==1:
                self.p0[c][...]=self.g[pl.ds(al(b+core*h),h),:]+self.r0[c][...]
                out=[self.send(self.p0[c].at[pl.ds(al(((co[dims[0]]+d)%4)*h4),h4)],self.r1[c].at[d-1],self.peer(dims[0],d)) for d in (2,1,3)]
            elif n==2:
                r=self.r1[c]
                self.p1[c][...]=(self.p0[c][pl.ds(al(co[dims[0]]*h4),h4),:]+r[0])+(r[1]+r[2])
                out=[self.send(self.p1[c].at[pl.ds(al(((co[dims[1]]+d)%4)*h16),h16)],self.r2[c].at[d-1],self.peer(dims[1],d)) for d in (2,1,3)]
            elif n==3:
                r=self.r2[c]; me=co[dims[2]]
                self.p2[c][me]=(self.p1[c][pl.ds(al(co[dims[1]]*h16),h16),:]+r[0])+(r[1]+r[2])
                out=[self.send(self.p2[c].at[me],self.p2[c].at[me],self.peer(dims[2],d)) for d in (2,1,3)]
            elif n==4:
                s=pl.ds(self.off(c,2),h16); t=self.p2[c]
                self.a[s,:]=(t[0]+t[1])+(t[2]+t[3])
                out=[self.send(self.a.at[s],self.a.at[s],self.peer(dims[1],d)) for d in (2,1,3)]
            elif n==5:
                s=pl.ds(self.off(c,1),h4)
                out=[self.send(self.a.at[s],self.a.at[s],self.peer(dims[0],d)) for d in (2,1,3)]
            elif n==6:
                s=pl.ds(self.off(c,0),h)
                out=[self.send(self.a.at[s],self.a.at[s],self.partner)]
            else: out=[]
            self.fly[c]=out

def body(cnt_ref,pi_ref,x_ref,v_ref,pr_ref,o_ref,y_ref,g,info,a,A,Rs,Li,Xs,Ys,*scr):
    s=pl.program_id(0)
    k6=lambda i: scr[6*i:6*i+6]
    cm=Comm(g,a,k6(0),k6(1),k6(2),k6(3),k6(4),k6(5),scr[36],scr[37])
    @pl.when(s==0)
    def _(): cm.greet()
    gram_part(s,cnt_ref,pi_ref,x_ref,v_ref,pr_ref,g,info)
    @pl.when(s==STEPS-1)
    def _(): rest(cm,o_ref,y_ref,a,A,Rs,Li,Xs,Ys)

def rest(cm,o_ref,y_ref,a,A,Rs,Li,Xs,Ys):
    P0=(0,1,2); P1=(3,4,5)
    cm.met()
    for n,cs in ((0,P0),(0,P1),(1,P0),(1,P1),(2,P0),(3,P0),(2,P1),(4,P0),(3,P1),(5,P0),(4,P1),(6,P0),(5,P1),(7,P0)): cm.step(n,cs)
    ii=lax.broadcasted_iota(jnp.int32,(8,128),0); jj=lax.broadcasted_iota(jnp.int32,(8,128),1)
    big=(128,128)
    l16=lax.broadcasted_iota(jnp.int32,(16,128),1)
    def unpack(base):
        e=a[base:base+16,:]; er=pltpu.roll(e,64,1)
        return [jnp.where(l16[:1]<64,e[2*k:2*k+1,:],er[2*k+1:2*k+2,:]) for k in range(8)]
    dg=unpack(80); dr=[lax.rsqrt(d) for d in dg]
    bl=[b*d for b,d in zip(unpack(64),dr)]
    a00=a[0:128,:]
    low=(lax.broadcasted_iota(jnp.int32,big,0)>=64)&(lax.broadcasted_iota(jnp.int32,big,1)<64)
    dc=[bc(d,big).T for d in dr]
    A[0:128,:]=jnp.where(low,a00.T,a00)*dc[0]*dr[0]
    def scale(k,j): A[blk(k,j),:]=a[blk(k,j),:]*dc[k]*dr[j]
    for j in range(1,8): scale(0,j)
    for j in range(1,5): scale(1,j)
    def factor(k):
        o=brow(k,k)
        R,I=factor_inplace2([A[o+8*p:o+8*p+8,:] for p in range(16)])
        for p in range(16):
            Rs[128*k+8*p:128*k+8*p+8,128*k:128*k+128]=jnp.where(jj>=ii+8*p,R[p],0.0)
            Li[8*p:8*p+8,:]=jnp.where(jj<8*p+8,I[p],0.0)
        if k: Rs[128*k:128*k+128,:128*k]=jnp.zeros((128,128*k),F32)
    def panel(k):
        Linv=Li[...]
        bk=jnp.concatenate([bl[k],jnp.zeros((7,128),F32)],axis=0)
        yk=lax.dot_general(bk,Linv,(((1,),(1,)),((),())),precision=lax.Precision.HIGHEST,preferred_element_type=F32)
        y_ref[k:k+1,:]=yk[0:1,:]
        n=7-k
        if n==0: return
        row_=jnp.concatenate([A[blk(k,j),:] for j in range(k+1,8)],axis=1)
        Rk=jnp.dot(lhs6(Linv),rhs6(row_),preferred_element_type=F32)
        Rs[128*k:128*k+128,128*(k+1):]=Rk
        Xs[0:16,:]=lhs6(jnp.concatenate([yk,jnp.zeros((8,128),F32)],axis=0))
        for i in range(n): Xs[16+128*i:144+128*i,:]=lhs6(Rk[:,128*i:128*i+128].T)
        Ys[:,:128*n]=rhs6(Rk)
    def update(k,j0,j1,i0,i1,withb):
        lo=0 if withb else 16+128*(i0-k-1)
        if withb and i0>k+1: X=jnp.concatenate([Xs[0:16,:],Xs[16+128*(i0-k-1):16+128*(i1-k-1),:]],axis=0)
        else: X=Xs[lo:16+128*(i1-k-1),:]
        D=jnp.dot(X,Ys[:,128*(j0-k-1):128*(j1-k-1)],preferred_element_type=F32)
        b0=16 if withb else 0
        for j in range(j0,j1):
            u=128*(j-j0)
            if withb: bl[j]=bl[j]-D[0:1,u:u+128]
            for i in range(i0,min(i1,j+1)):
                z=b0+128*(i-i0)
                A[blk(i,j),:]=A[blk(i,j),:]-D[z:z+128,u:u+128]
    factor(0)
    cm.step(6,P1)
    panel(0)
    update(0,1,5,1,2,True)
    factor(1)
    cm.step(7,P1)
    for k in range(1,8):
        for j in range(max(k,5) if k==1 else k,8): scale(k,j)
    update(0,5,8,1,8,True)
    update(0,2,3,2,3,False)
    update(0,3,5,2,5,False)
    for k in range(1,8):
        panel(k)
        if k==7: break
        for j in range(k+1,8,2): update(k,j,min(j+2,8),k+1,min(j+2,8),True)
        factor(k+1)
    s=pl.multiple_of(cm.q*64,64)
    for j in range(8):
        o_ref[:,128*j:128*j+128]=Rs[pl.ds(s,64),128*j:128*j+128]*(dg[j]*dr[j])

def local(readings,values,counts,prior_root,prior_info):
    V=lambda *s: pltpu.VMEM(s,F32)
    H=HALF
    scr=[V(ROWS,128),V(8,128),V(ROWS,128),V(ROWS,128),V(NS,NS),V(128,128),pltpu.VMEM((16+7*128,768),BF),pltpu.VMEM((768,896),BF)]
    scr+=[V(h,128) for h in H]+[V(3,h//4,128) for h in H]+[V(3,h//16,128) for h in H]+[V(h,128) for h in H]+[V(h//4,128) for h in H]+[V(4,h//16,128) for h in H]
    scr+=[pltpu.SemaphoreType.DMA((102,)),pltpu.SemaphoreType.DMA((102,))]
    smem=pl.BlockSpec(memory_space=pltpu.SMEM)
    root,y=pl.pallas_call(body,grid=(STEPS,),
        in_specs=[smem,smem,pl.BlockSpec((CH,NS),lambda s:(s,0)),pl.BlockSpec((CAP//128,128),lambda s:(0,0)),pl.BlockSpec((8,NS),lambda s:(0,0))],
        out_specs=(pl.BlockSpec((64,NS),lambda s:(0,0)),pl.BlockSpec((8,128),lambda s:(0,0))),
        out_shape=(jax.ShapeDtypeStruct((64,NS),F32),jax.ShapeDtypeStruct((8,128),F32)),
        scratch_shapes=scr,
        compiler_params=pltpu.CompilerParams(collective_id=0,has_side_effects=True,vmem_limit_bytes=58*2**20),
    )(counts,prior_info,readings,values.reshape(CAP//128,128),prior_root)
    return root,y.reshape(NS)
from jax.sharding import PartitionSpec as P
def solution(mesh):
    placed=(P(("fibre","blk"),None),P(("fibre","blk")),P(("fibre","blk")),P(("fibre","blk"),None),P(("fibre","blk")))
    return jax.shard_map(local,mesh=mesh,in_specs=placed,out_specs=(P("blk",None),P()),check_vma=False)
```

time: 81.1 us -> 75.4 us (0.930)
  Pallas kernels: 78 us -> 71 us
  local copies, waits for them, and re-layouts: 1.7 us -> 2.95 us
    pallas_call x3 -> x1, Pallas kernels: 78 us -> 71 us  [local(): pl.pallas_call(body, grid=(STEPS,), in_specs=[smem, smem, pl.BlockSpec((C...]
    unnamed x2, local copies, waits for them, and re-layouts: 1.7 us -> 2.95 us
where the time goes in v3:
time: 75.4 us; the launch traced here: 75.2 us
  Pallas kernels  71 us (94%)
  local copies, waits for them, and re-layouts  2.95 us (4%)
  between operations  1.28 us (2%)
    pallas_call x1, Pallas kernels, local(): pl.pallas_call(body, grid=(STEPS,), in_specs=[smem, smem, pl.BlockSpec((C...  71 us
    unnamed x2, local copies, waits for them, and re-layouts  2.95 us

profile of v3, /device:TPU:1, one launch (start us, length us, event | category | flops | bytes accessed | tf_op | source)
XLA Modules:
  0.0 75.2 jit_solution(2608269511035226297)
XLA Ops:
  1.3 71.0 %shard_map.68 = (f32[64,1024]{1,0:T(8,128)}, f32[8,128]{1,0:T(8,128)}) custom-call(s32[1]{0:T(128)S(6)} %copy.9.cnt_ref, f32[8]{0:T(128)} %pi_ref.1, bf16[4096,1024]{1,0:T(8,128)(2,1)} %x_ref.1, bf16[32,128]{1,0:T(8,128)(2,1)} %bitcast.2, f32[8,1024]{1,0:T(8,128)} %pr_ref.1), custom_call_target="tpu_custom_call" | custom-call | tf_op jit(solution)/shard_map/pallas_call | solution.py:378
  72.3 1.7 %copy.10 = f32[64,1024]{1,0:T(8,128)} copy(f32[64,1024]{1,0:T(8,128)} %get-tuple-element.8) | data formatting | bytes 524288
  73.9 1.3 %copy.11 = f32[1024]{0:T(1024)} copy(f32[1024]{0:T(1024)} %bitcast.3) | data formatting | bytes 8192

commit v4 on v3

--- a/solution.py
+++ b/solution.py
@@ -106,22 +106,25 @@
 def split3(x):
     h=x.astype(BF).astype(F32); r=x-h; m=r.astype(BF).astype(F32); l=r-m
     return h,m,l
-def outer6(x):
-    h,m,l=split3(x)
+def outer6(xs,lo,lane):
+    n=len(xs)
+    x=jnp.concatenate(xs,axis=0)
+    z=jnp.concatenate([t if i==n-1 else jnp.where((lane>=lo-8*(n-2-i))&(lane<lo+8),0.0,t) for i,t in enumerate(xs)],axis=0)
+    h,m,l=split3(x); zh,zm,zl=split3(z)
     a=jnp.concatenate([h,h,m,m,h,l],axis=0)
-    b=jnp.concatenate([h,m,h,m,l,h],axis=0).astype(BF)
+    b=jnp.concatenate([zh,zm,zh,zm,zl,zh],axis=0).astype(BF)
     return jnp.dot(a.T.astype(BF),b,preferred_element_type=F32)
-def factor_inplace2(T,G=3,order="mxu"):
+def factor_inplace2(T,G=3,B=2):
     T=list(T)
     sub=lax.broadcasted_iota(jnp.int32,(8,128),0); lane=lax.broadcasted_iota(jnp.int32,(8,128),1)
     R=[];I=[]
     C=[col(T[0],c) for c in range(8)]
     for p in range(16):
         lo=8*p
-        inpan=(lane>=lo)&(lane<lo+8)
+        inpan=(lane>=lo)&(lane<lo+8); inbat=(lane>=lo-8*(p%B))&(lane<lo+8)
         VA=T[p]
         VX=jnp.where(inpan,jnp.where(lane==sub+lo,1.0,0.0),T[p])
-        near=range(p+1,min(p+1+G,16)); far=range(p+1+G,16)
+        end=min(p-p%B+B+G,16); near=range(p+1,end); far=range(end,16) if p%B==B-1 else ()
         Q={q:[col(T[q],lo+c) for c in range(8)] for q in near}
         Cn=[col(T[p+1],lo+8+c) for c in range(8)] if p<15 else None
         LQ={q:[] for q in near}; RX=[]
@@ -160,7 +163,7 @@
         R.append(jnp.where(lane<lo+8,oA,oX)); I.append(oX)
         if p<15:
             if len(far):
-                D=outer6(oX)
+                D=outer6(I[-B:],lo,lane)
             for q in near:
                 t=jnp.where(inpan,0.0,T[q])
                 for j in range(8): t=t-LQ[q][j]*RX[j]
@@ -171,10 +174,10 @@
                 Cn[k]=t
             C=Cn
             for q in far:
-                T[q]=jnp.where(inpan,0.0,T[q])-D[8*q:8*q+8,:]
+                T[q]=jnp.where(inbat,0.0,T[q])-D[8*q:8*q+8,:]
     return R,I
 MESH=pl.DeviceIdType.MESH
-NS=1024; CAP=4096; CH=1024; STEPS=CAP//CH; ROWS=4608
+NS=1024; CAP=4096; ROWS=4608; SLABS=(512,512,1024,1024,1024)
 PIECES=((0,512,(0,1,2)),(512,512,(1,2,0)),(1024,512,(2,0,1)),(1536,1024,(0,1,2)),(2560,1024,(1,2,0)),(3584,1024,(2,0,1)))
 HALF=[n//2 for _,n,_ in PIECES]
 def split3b(x):
@@ -187,47 +190,46 @@
 def brow(k,j): return 128*(8*k-k*(k-1)//2+(j-k))
 def blk(k,j): return pl.ds(brow(k,j),128)
 
-def gram_part(s,cnt_ref,pi_ref,x_ref,v_ref,pr_ref,g,info):
-    x=x_ref[...]
-    rowi=lax.broadcasted_iota(jnp.int32,(CH,NS),0)+s*CH
-    xm=jnp.where(rowi<cnt_ref[0],x,jnp.zeros((),BF))
-    xt=x.T
-    vf=v_ref[pl.ds(pl.multiple_of(s*(CH//128),8),CH//128),:].astype(F32)
-    v=jnp.broadcast_to(jnp.concatenate([vf[i:i+1,:] for i in range(CH//128)],axis=1),(16,CH)).astype(BF)
-    def accum(first,xt,v,xm):
-        lhs=jnp.concatenate([v,xt],axis=0)
+def gram_part(cnt_ref,pi_ref,x_hbm,v_ref,pr_ref,g,info,xb,xsem):
+    cps=[]; at=0
+    for i,n in enumerate(SLABS):
+        cp=pltpu.make_async_copy(x_hbm.at[pl.ds(at,n)],xb.at[pl.ds(at,n)],xsem.at[i]); cp.start()
+        cps.append((cp,at,n)); at+=n
+    def accum(first,lhs,rhs,v):
+        Dv=jnp.dot(v,rhs,preferred_element_type=F32)
+        for j in range(8):
+            dv=Dv[0:1,128*j:128*j+128]
+            info[j:j+1,:]=dv if first else info[j:j+1,:]+dv
         for c in range(4):
-            D=jnp.dot(lhs[:16+256*(c+1)],xm[:,256*c:256*c+256],preferred_element_type=F32)
+            D=lax.dot_general(lhs[:,:256*(c+1)],rhs[:,256*c:256*c+256],(((0,),(0,)),((),())),preferred_element_type=F32)
             for u in range(2):
                 j=2*c+u
-                dv=D[0:1,128*u:128*u+128]
-                info[j:j+1,:]=dv if first else info[j:j+1,:]+dv
                 for i in range(j+1):
-                    z=16+128*i; d=D[z:z+128,128*u:128*u+128]
+                    d=D[128*i:128*i+128,128*u:128*u+128]
                     g[blk(i,j),:]=d if first else g[blk(i,j),:]+d
-    @pl.when(s==0)
-    def _(): accum(True,xt,v,xm)
-    @pl.when(s>0)
-    def _(): accum(False,xt,v,xm)
-    @pl.when(s==STEPS-1)
-    def _():
-        sub=lax.broadcasted_iota(jnp.int32,(8,128),0)
-        pv=jnp.zeros((8,128),F32)
-        for i in range(8): pv=jnp.where(sub==i,pi_ref[i],pv)
-        h,m,l=split3(jnp.concatenate([pr_ref[...],pv],axis=1))
-        z=jnp.zeros((80,NS+128),F32)
-        a=jnp.concatenate([h,h,m,m,h,l,z],axis=0)
-        b=jnp.concatenate([h,m,h,m,l,h,z],axis=0)[:,:NS].astype(BF)
-        at=a.T.astype(BF)
-        accum(False,at[:NS],at[NS:NS+16],b)
-        eye=lax.broadcasted_iota(jnp.int32,(128,128),0)==lax.broadcasted_iota(jnp.int32,(128,128),1)
-        lane=lax.broadcasted_iota(jnp.int32,(1,128),1)
-        for k in range(8):
-            dg=jnp.sum(jnp.where(eye,g[blk(k,k),:],0.0),axis=0,keepdims=True)
-            for base,r in ((64,info[k:k+1,:]),(80,dg)):
-                rr=pltpu.roll(jnp.broadcast_to(r,(8,128)),64,1)[0:1,:]
-                g[base+2*k:base+2*k+1,:]=jnp.where(lane<64,r,g[base+2*k:base+2*k+1,:])
-                g[base+2*k+1:base+2*k+2,:]=jnp.where(lane<64,rr,g[base+2*k+1:base+2*k+2,:])
+    sub=lax.broadcasted_iota(jnp.int32,(8,128),0)
+    pv=jnp.zeros((8,128),F32)
+    for i in range(8): pv=jnp.where(sub==i,pi_ref[i],pv)
+    h,m,l=split3(jnp.concatenate([pr_ref[...],pv],axis=1))
+    z=jnp.zeros((80,NS+128),F32)
+    pa=jnp.concatenate([h,h,m,m,h,l,z],axis=0)
+    pb=jnp.concatenate([h,m,h,m,l,h,z],axis=0)[:,:NS].astype(BF)
+    accum(True,pa[:,:NS].astype(BF),pb,pa[:,NS:].T[:16].astype(BF))
+    for cp,at,n in cps:
+        cp.wait()
+        x=xb[pl.ds(at,n),:]
+        xm=jnp.where(lax.broadcasted_iota(jnp.int32,(n,NS),0)+at<cnt_ref[0],x,jnp.zeros((),BF))
+        vf=v_ref[at//128:(at+n)//128,:].astype(F32)
+        v=jnp.broadcast_to(jnp.concatenate([vf[i:i+1,:] for i in range(n//128)],axis=1),(16,n)).astype(BF)
+        accum(False,x,xm,v)
+    eye=lax.broadcasted_iota(jnp.int32,(128,128),0)==lax.broadcasted_iota(jnp.int32,(128,128),1)
+    lane=lax.broadcasted_iota(jnp.int32,(1,128),1)
+    for k in range(8):
+        dg=jnp.sum(jnp.where(eye,g[blk(k,k),:],0.0),axis=0,keepdims=True)
+        for base,r in ((64,info[k:k+1,:]),(80,dg)):
+            rr=pltpu.roll(jnp.broadcast_to(r,(8,128)),64,1)[0:1,:]
+            g[base+2*k:base+2*k+1,:]=jnp.where(lane<64,r,g[base+2*k:base+2*k+1,:])
+            g[base+2*k+1:base+2*k+2,:]=jnp.where(lane<64,rr,g[base+2*k+1:base+2*k+2,:])
 
 class Comm:
     def __init__(self,g,a,r0,r1,r2,p0,p1,p2,ssem,rsem):
@@ -287,15 +289,12 @@
             else: out=[]
             self.fly[c]=out
 
-def body(cnt_ref,pi_ref,x_ref,v_ref,pr_ref,o_ref,y_ref,g,info,a,A,Rs,Li,Xs,Ys,*scr):
-    s=pl.program_id(0)
+def body(cnt_ref,pi_ref,x_hbm,v_ref,pr_ref,o_ref,y_ref,xb,xsem,g,info,a,A,Rs,Li,Xs,Ys,*scr):
     k6=lambda i: scr[6*i:6*i+6]
     cm=Comm(g,a,k6(0),k6(1),k6(2),k6(3),k6(4),k6(5),scr[36],scr[37])
-    @pl.when(s==0)
-    def _(): cm.greet()
-    gram_part(s,cnt_ref,pi_ref,x_ref,v_ref,pr_ref,g,info)
-    @pl.when(s==STEPS-1)
-    def _(): rest(cm,o_ref,y_ref,a,A,Rs,Li,Xs,Ys)
+    cm.greet()
+    gram_part(cnt_ref,pi_ref,x_hbm,v_ref,pr_ref,g,info,xb,xsem)
+    rest(cm,o_ref,y_ref,a,A,Rs,Li,Xs,Ys)
 
 def rest(cm,o_ref,y_ref,a,A,Rs,Li,Xs,Ys):
     P0=(0,1,2); P1=(3,4,5)
@@ -318,7 +317,7 @@
     for j in range(1,5): scale(1,j)
     def factor(k):
         o=brow(k,k)
-        R,I=factor_inplace2([A[o+8*p:o+8*p+8,:] for p in range(16)])
+        R,I=factor_inplace2(G=1,B=5,T=[A[o+8*p:o+8*p+8,:] for p in range(16)])
         for p in range(16):
             Rs[128*k+8*p:128*k+8*p+8,128*k:128*k+128]=jnp.where(jj>=ii+8*p,R[p],0.0)
             Li[8*p:8*p+8,:]=jnp.where(jj<8*p+8,I[p],0.0)
@@ -368,20 +367,25 @@
     for j in range(8):
         o_ref[:,128*j:128*j+128]=Rs[pl.ds(s,64),128*j:128*j+128]*(dg[j]*dr[j])
 
+def finish(o_in,y_in,o_ref,y_ref):
+    o_ref[...]=o_in[...]
+    y_ref[...]=y_in[...]
+
 def local(readings,values,counts,prior_root,prior_info):
     V=lambda *s: pltpu.VMEM(s,F32)
     H=HALF
-    scr=[V(ROWS,128),V(8,128),V(ROWS,128),V(ROWS,128),V(NS,NS),V(128,128),pltpu.VMEM((16+7*128,768),BF),pltpu.VMEM((768,896),BF)]
+    scr=[pltpu.VMEM((CAP,NS),BF),pltpu.SemaphoreType.DMA((len(SLABS),))]
+    scr+=[V(ROWS,128),V(8,128),V(ROWS,128),V(ROWS,128),V(NS,NS),V(128,128),pltpu.VMEM((16+7*128,768),BF),pltpu.VMEM((768,896),BF)]
     scr+=[V(h,128) for h in H]+[V(3,h//4,128) for h in H]+[V(3,h//16,128) for h in H]+[V(h,128) for h in H]+[V(h//4,128) for h in H]+[V(4,h//16,128) for h in H]
     scr+=[pltpu.SemaphoreType.DMA((102,)),pltpu.SemaphoreType.DMA((102,))]
-    smem=pl.BlockSpec(memory_space=pltpu.SMEM)
-    root,y=pl.pallas_call(body,grid=(STEPS,),
-        in_specs=[smem,smem,pl.BlockSpec((CH,NS),lambda s:(s,0)),pl.BlockSpec((CAP//128,128),lambda s:(0,0)),pl.BlockSpec((8,NS),lambda s:(0,0))],
-        out_specs=(pl.BlockSpec((64,NS),lambda s:(0,0)),pl.BlockSpec((8,128),lambda s:(0,0))),
-        out_shape=(jax.ShapeDtypeStruct((64,NS),F32),jax.ShapeDtypeStruct((8,128),F32)),
-        scratch_shapes=scr,
+    smem=pl.BlockSpec(memory_space=pltpu.SMEM); vmem=pl.BlockSpec(memory_space=pltpu.VMEM)
+    outs=(jax.ShapeDtypeStruct((64,NS),F32),jax.ShapeDtypeStruct((8,128),F32))
+    root,y=pl.pallas_call(body,
+        in_specs=[smem,smem,pl.BlockSpec(memory_space=pl.ANY),vmem,vmem],
+        out_specs=(vmem,vmem),out_shape=outs,scratch_shapes=scr,
         compiler_params=pltpu.CompilerParams(collective_id=0,has_side_effects=True,vmem_limit_bytes=58*2**20),
     )(counts,prior_info,readings,values.reshape(CAP//128,128),prior_root)
+    root,y=pl.pallas_call(finish,in_specs=[vmem,vmem],out_specs=(vmem,vmem),out_shape=outs)(root,y)
     return root,y.reshape(NS)
 from jax.sharding import PartitionSpec as P
 def solution(mesh):

time: 75.4 us -> 71.2 us (0.944)
  local copies, waits for them, and re-layouts: 2.95 us -> 0 us
  Pallas kernels: 71 us -> 69.7 us
    unnamed x2 -> x0, local copies, waits for them, and re-layouts: 2.95 us -> none
    pallas_call x1 -> x2, Pallas kernels: 71 us -> 69.7 us  [the longest x1 68.1 us: local(): pl.pallas_call(body, in_specs=[smem, smem, pl.BlockSpec(memory_space=pl.A...]
where the time goes in v4:
time: 71.2 us; the launch traced here: 71 us
  Pallas kernels  69.7 us (98%)
  between operations  1.29 us (2%)
    pallas_call x1, Pallas kernels, local(): pl.pallas_call(body, in_specs=[smem, smem, pl.BlockSpec(memory_space=pl.A...  68.1 us
    pallas_call x1, Pallas kernels, local(): pl.pallas_call(finish, in_specs=[vmem, vmem], out_specs=(vmem, vmem), out...  1.68 us

profile of v4, /device:TPU:1, one launch (start us, length us, event | category | flops | bytes accessed | tf_op | source)
XLA Modules:
  0.0 71.0 jit_solution(4754331591433847286)
XLA Ops:
  1.3 68.1 %shard_map.68 = (f32[64,1024]{1,0:T(8,128)}, f32[8,128]{1,0:T(8,128)}) custom-call(s32[1]{0:T(128)S(6)} %copy.7.cnt_ref, f32[8]{0:T(128)} %pi_ref.1, bf16[4096,1024]{1,0:T(8,128)(2,1)} %x_hbm.1, bf16[32,128]{1,0:T(8,128)(2,1)} %bitcast.2, f32[8,1024]{1,0:T(8,128)} %pr_ref.1), custom_call_target="tpu_custom_call" | custom-call | tf_op jit(solution)/shard_map/pallas_call | solution.py:383
  69.3 1.7 %shard_map.69 = (f32[64,1024]{1,0:T(8,128)}, f32[8,128]{1,0:T(8,128)}) custom-call(f32[64,1024]{1,0:T(8,128)} %get-tuple-element.6.o_in, f32[8,128]{1,0:T(8,128)} %get-tuple-element.7.y_in), custom_call_target="tpu_custom_call" | custom-call | tf_op jit(solution)/shard_map/pallas_call | solution.py:388

commit v5 on v4

--- a/solution.py
+++ b/solution.py
@@ -261,6 +261,7 @@
         al=lambda v: pl.multiple_of(v,8)
         for c in cs:
             b,_,dims=PIECES[c]; h=HALF[c]; h4=h//4; h16=h//16
+            if n==5 and c<3: continue
             for x in self.fly.pop(c,()): x.wait()
             core,co=self.core,self.co
             if n==0:
@@ -268,6 +269,18 @@
             elif n==1:
                 self.p0[c][...]=self.g[pl.ds(al(b+core*h),h),:]+self.r0[c][...]
                 out=[self.send(self.p0[c].at[pl.ds(al(((co[dims[0]]+d)%4)*h4),h4)],self.r1[c].at[d-1],self.peer(dims[0],d)) for d in (2,1,3)]
+            elif n==2 and c<3:
+                r=self.r1[c]; me=co[dims[1]]
+                self.r2[c][me]=(self.p0[c][pl.ds(al(co[dims[0]]*h4),h4),:]+r[0])+(r[1]+r[2])
+                out=[self.send(self.r2[c].at[me],self.r2[c].at[me],self.peer(dims[1],d)) for d in (2,1,3)]
+            elif n==3 and c<3:
+                t=self.r2[c]; me=co[dims[2]]
+                self.p2[c][me]=(t[0]+t[1])+(t[2]+t[3])
+                out=[self.send(self.p2[c].at[me],self.p2[c].at[me],self.peer(dims[2],d)) for d in (2,1,3)]
+            elif n==4 and c<3:
+                s=pl.ds(self.off(c,1),h4); t=self.p2[c]
+                self.a[s,:]=(t[0]+t[1])+(t[2]+t[3])
+                out=[self.send(self.a.at[s],self.a.at[s],self.peer(dims[0],d)) for d in (2,1,3)]
             elif n==2:
                 r=self.r1[c]
                 self.p1[c][...]=(self.p0[c][pl.ds(al(co[dims[0]]*h4),h4),:]+r[0])+(r[1]+r[2])
@@ -299,7 +312,7 @@
 def rest(cm,o_ref,y_ref,a,A,Rs,Li,Xs,Ys):
     P0=(0,1,2); P1=(3,4,5)
     cm.met()
-    for n,cs in ((0,P0),(0,P1),(1,P0),(1,P1),(2,P0),(3,P0),(2,P1),(4,P0),(3,P1),(5,P0),(4,P1),(6,P0),(5,P1),(7,P0)): cm.step(n,cs)
+    for n,cs in ((0,P0),(0,P1),(1,P0),(1,P1),(2,P0),(2,P1),(3,P0),(3,P1),(4,P0),(4,P1),(6,P0),(5,P1),(7,P0)): cm.step(n,cs)
     ii=lax.broadcasted_iota(jnp.int32,(8,128),0); jj=lax.broadcasted_iota(jnp.int32,(8,128),1)
     big=(128,128)
     l16=lax.broadcasted_iota(jnp.int32,(16,128),1)
@@ -376,7 +389,7 @@
     H=HALF
     scr=[pltpu.VMEM((CAP,NS),BF),pltpu.SemaphoreType.DMA((len(SLABS),))]
     scr+=[V(ROWS,128),V(8,128),V(ROWS,128),V(ROWS,128),V(NS,NS),V(128,128),pltpu.VMEM((16+7*128,768),BF),pltpu.VMEM((768,896),BF)]
-    scr+=[V(h,128) for h in H]+[V(3,h//4,128) for h in H]+[V(3,h//16,128) for h in H]+[V(h,128) for h in H]+[V(h//4,128) for h in H]+[V(4,h//16,128) for h in H]
+    scr+=[V(h,128) for h in H]+[V(3,h//4,128) for h in H]+[V(4,h//4,128) if i<3 else V(3,h//16,128) for i,h in enumerate(H)]+[V(h,128) for h in H]+[V(h//4,128) for h in H]+[V(4,h//4 if i<3 else h//16,128) for i,h in enumerate(H)]
     scr+=[pltpu.SemaphoreType.DMA((102,)),pltpu.SemaphoreType.DMA((102,))]
     smem=pl.BlockSpec(memory_space=pltpu.SMEM); vmem=pl.BlockSpec(memory_space=pltpu.VMEM)
     outs=(jax.ShapeDtypeStruct((64,NS),F32),jax.ShapeDtypeStruct((8,128),F32))

time: 71.2 us -> 68.7 us (0.965); the launches traced: 71 us -> 67.8 us
  Pallas kernels: 69.7 us -> 66.5 us
    pallas_call x1, Pallas kernels: 68.1 us -> 64.8 us  [local(): pl.pallas_call(body, in_specs=[smem, smem, pl.BlockSpec(memory_space=pl.A...]
where the time goes in v5:
time: 68.7 us; the launch traced here: 67.8 us
  Pallas kernels  66.5 us (97%)
  between operations  1.29 us (2%)
    pallas_call x1, Pallas kernels, local(): pl.pallas_call(body, in_specs=[smem, smem, pl.BlockSpec(memory_space=pl.A...  64.8 us
    pallas_call x1, Pallas kernels, local(): pl.pallas_call(finish, in_specs=[vmem, vmem], out_specs=(vmem, vmem), out...  1.68 us

profile of v5, /device:TPU:1, one launch (start us, length us, event | category | flops | bytes accessed | tf_op | source)
XLA Modules:
  0.0 67.8 jit_solution(11789400822206330731)
XLA Ops:
  1.3 64.8 %shard_map.68 = (f32[64,1024]{1,0:T(8,128)}, f32[8,128]{1,0:T(8,128)}) custom-call(s32[1]{0:T(128)S(6)} %copy.7.cnt_ref, f32[8]{0:T(128)} %pi_ref.1, bf16[4096,1024]{1,0:T(8,128)(2,1)} %x_hbm.1, bf16[32,128]{1,0:T(8,128)(2,1)} %bitcast.2, f32[8,1024]{1,0:T(8,128)} %pr_ref.1), custom_call_target="tpu_custom_call" | custom-call | tf_op jit(solution)/shard_map/pallas_call | solution.py:396
  66.1 1.7 %shard_map.69 = (f32[64,1024]{1,0:T(8,128)}, f32[8,128]{1,0:T(8,128)}) custom-call(f32[64,1024]{1,0:T(8,128)} %get-tuple-element.6.o_in, f32[8,128]{1,0:T(8,128)} %get-tuple-element.7.y_in), custom_call_target="tpu_custom_call" | custom-call | tf_op jit(solution)/shard_map/pallas_call | solution.py:401

commit v6 on v5

--- a/solution.py
+++ b/solution.py
@@ -361,9 +361,9 @@
                 z=b0+128*(i-i0)
                 A[blk(i,j),:]=A[blk(i,j),:]-D[z:z+128,u:u+128]
     factor(0)
-    cm.step(6,P1)
     panel(0)
     update(0,1,5,1,2,True)
+    cm.step(6,P1)
     factor(1)
     cm.step(7,P1)
     for k in range(1,8):

time: 68.7 us -> 67.9 us (0.988)
  no operation moved by 1% of the time
where the time goes in v6:
time: 67.9 us; the launch traced here: 67.7 us
  Pallas kernels  66.4 us (98%)
  between operations  1.29 us (2%)
    pallas_call x1, Pallas kernels, local(): pl.pallas_call(body, in_specs=[smem, smem, pl.BlockSpec(memory_space=pl.A...  64.7 us
    pallas_call x1, Pallas kernels, local(): pl.pallas_call(finish, in_specs=[vmem, vmem], out_specs=(vmem, vmem), out...  1.68 us

profile of v6, /device:TPU:1, one launch (start us, length us, event | category | flops | bytes accessed | tf_op | source)
XLA Modules:
  0.0 67.7 jit_solution(13291482645878526544)
XLA Ops:
  1.3 64.7 %shard_map.68 = (f32[64,1024]{1,0:T(8,128)}, f32[8,128]{1,0:T(8,128)}) custom-call(s32[1]{0:T(128)S(6)} %copy.7.cnt_ref, f32[8]{0:T(128)} %pi_ref.1, bf16[4096,1024]{1,0:T(8,128)(2,1)} %x_hbm.1, bf16[32,128]{1,0:T(8,128)(2,1)} %bitcast.2, f32[8,1024]{1,0:T(8,128)} %pr_ref.1), custom_call_target="tpu_custom_call" | custom-call | tf_op jit(solution)/shard_map/pallas_call | solution.py:396
  66.0 1.7 %shard_map.69 = (f32[64,1024]{1,0:T(8,128)}, f32[8,128]{1,0:T(8,128)}) custom-call(f32[64,1024]{1,0:T(8,128)} %get-tuple-element.6.o_in, f32[8,128]{1,0:T(8,128)} %get-tuple-element.7.y_in), custom_call_target="tpu_custom_call" | custom-call | tf_op jit(solution)/shard_map/pallas_call | solution.py:401
